TPU v7x, 256 devices: a whole 4x4x8 slice. The times are simulated.
256 devices in a mesh: seq: 64 (over z, y, core), head: 4 (over x).
Axes of the slice: x: 4, y: 4, z: 8, core: 2. Of those that a mesh axis runs over, the one named last changes fastest.
Arguments:
- queries: bfloat16 [49152, 4096], P(('seq', 'head')), may hold values from -6 to 6
- key_rows: bfloat16 [49152, 4096], P(('seq', 'head')), may hold values from -6 to 6
- values: bfloat16 [49152, 4096], P(('seq', 'head')), may hold values from -6 to 6
- doc_ids: int32 [49152], replicated, may hold values from 0 to 127, as said below
- image_flags: int32 [49152], replicated, may hold values from 0 to 1, as said below
- labels: int32 [49152], P(('seq', 'head')), may hold values from -1 to 31999, as said below
- token_loss: float32 [49152], P(('seq', 'head')), may hold values from 0.05 to 8
Outputs:
- attended: bfloat16 [49152, 4096], P(('seq', 'head'))
- doc_count: float32 [128], replicated
- doc_loss: float32 [128], replicated
Inputs may be any that keep to these rules, and one draw needn't show every extreme that they name: `doc_ids`: document numbers never fall along the sequence and rise by one from one document to the next; every document holds at least 64 and at most 704 tokens, and some document holds exactly 704. `image_flags`: the 1s form spans of exactly 576 consecutive tokens, at most one span a document, each inside one document and never at its first token. `labels`: every image token has -1, and some document has -1 on all of its tokens.
All inputs are finite; a program needn't handle non-finite values.
Results may differ from a plain program's by a relative error of at most 0.0034.
Values may be sent and summed in bfloat16 or wider, within the bound.
A program may use at most 128 MiB of HBM per device.

v0:
```python
import functools

import jax
import jax.numpy as jnp
from jax import lax
from jax.sharding import Mesh
from jax.sharding import PartitionSpec as P

HEAD_DIM = 128
TOK_DEV = 768
DOC_MEAN = 384
DOC_MOST = 704
IMG_LEN = 576
SEQ = ("seq_0", "seq_1", "seq_2")
SEQ_HEAD = ("seq_0", "seq_1", "seq_2", "head")


def shifted(block, axis, distance):
    devices = range(lax.axis_size(axis))
    route = [(i - distance, i) for i in devices if i - distance in devices]
    return lax.ppermute(block, axis, route)


def over_axes(value, axes):
    return functools.reduce(lax.psum, axes, value)


def cut_rows(reach):
    return min(TOK_DEV, -(-reach // 128) * 128)


def allowed_pairs(query_docs, query_flags, query_places, key_docs, key_flags, key_places):
    same = query_docs[:, None] == key_docs[None, :]
    earlier = key_places[None, :] <= query_places[:, None]
    image = (query_flags[:, None] == 1) & (key_flags[None, :] == 1)
    return same & (earlier | image)


def attend(query_part, key_window, value_window, allowed):
    outputs = []
    scale = HEAD_DIM ** (-0.5)
    for head_index in range(query_part.shape[1] // HEAD_DIM):
        lower = head_index * HEAD_DIM
        query_head = query_part[:, lower : lower + HEAD_DIM]
        key_head = key_window[:, lower : lower + HEAD_DIM]
        value_head = value_window[:, lower : lower + HEAD_DIM]
        scores = (
            lax.dot_general(
                query_head, key_head, (((1,), (1,)), ((), ())), preferred_element_type=jnp.float32
            )
            * scale
        )
        scores = jnp.where(allowed, scores, -jnp.inf)
        row_max = jnp.max(scores, axis=1, keepdims=True)
        weights = jnp.exp(scores - row_max)
        total = jnp.sum(weights, axis=1, keepdims=True)
        mixed = (
            jnp.dot(weights.astype(jnp.bfloat16), value_head, preferred_element_type=jnp.float32)
            / total
        )
        outputs.append(mixed.astype(jnp.bfloat16))
    return jnp.concatenate(outputs, axis=1)


def per_device(queries, key_rows, values, doc_ids, image_flags, labels, token_loss):
    query_local, key_local, value_local = (
        lax.all_to_all(queries, "head", split_axis=1, concat_axis=0, tiled=True),
        lax.all_to_all(key_rows, "head", split_axis=1, concat_axis=0, tiled=True),
        lax.all_to_all(values, "head", split_axis=1, concat_axis=0, tiled=True),
    )
    reach_back = (DOC_MOST + TOK_DEV - 2) // TOK_DEV
    reach_front = (IMG_LEN + TOK_DEV - 2) // TOK_DEV
    behind = [shifted((key_local, value_local), SEQ, 1)]
    ahead = [
        shifted(
            (
                key_local[: cut_rows(IMG_LEN - 1 - (1 - 1) * TOK_DEV)],
                value_local[: cut_rows(IMG_LEN - 1 - (1 - 1) * TOK_DEV)],
            ),
            SEQ,
            -1,
        )
    ]
    key_window = jnp.concatenate(
        [pair[0] for pair in behind] + [key_local] + [pair[0] for pair in ahead], axis=0
    )
    value_window = jnp.concatenate(
        [pair[1] for pair in behind] + [value_local] + [pair[1] for pair in ahead], axis=0
    )
    back_total = sum((pair[0].shape[0] for pair in behind))
    window_rows = key_window.shape[0]
    block_start = lax.axis_index(SEQ) * TOK_DEV
    pad_front = reach_back * TOK_DEV
    pad_back = reach_front * TOK_DEV
    padded_docs = jnp.pad(doc_ids, (pad_front, pad_back), constant_values=-1)
    padded_flags = jnp.pad(image_flags, (pad_front, pad_back))
    key_docs = lax.dynamic_slice_in_dim(
        padded_docs, block_start + pad_front - back_total, window_rows
    )
    key_flags = lax.dynamic_slice_in_dim(
        padded_flags, block_start + pad_front - back_total, window_rows
    )
    query_docs = lax.dynamic_slice_in_dim(doc_ids, block_start, TOK_DEV)
    query_flags = lax.dynamic_slice_in_dim(image_flags, block_start, TOK_DEV)
    query_places = block_start + jnp.arange(TOK_DEV, dtype=jnp.int32)
    key_places = block_start - back_total + jnp.arange(window_rows, dtype=jnp.int32)
    allowed = allowed_pairs(query_docs, query_flags, query_places, key_docs, key_flags, key_places)
    attended = attend(query_local, key_window, value_window, allowed)
    output = lax.all_to_all(attended, "head", split_axis=0, concat_axis=1, tiled=True)
    local_rows = labels.shape[0]
    row_start = (lax.axis_index(SEQ) * lax.axis_size("head") + lax.axis_index("head")) * local_rows
    local_docs = lax.dynamic_slice_in_dim(doc_ids, row_start, local_rows)
    documents = doc_ids.shape[0] // DOC_MEAN
    member = (local_docs[:, None] == jnp.arange(documents, dtype=jnp.int32)[None, :]) & (
        labels[:, None] >= 0
    )
    counts = jnp.sum(member.astype(jnp.float32), axis=0)
    sums = jnp.sum(jnp.where(member, token_loss[:, None], jnp.float32(0.0)), axis=0)
    counts, sums = (over_axes(counts, SEQ_HEAD), over_axes(sums, SEQ_HEAD))
    return (output, counts, sums / jnp.maximum(counts, jnp.float32(1.0)))


def solution(mesh):
    split = Mesh(
        mesh.devices.reshape(8, 4, 2, mesh.shape["head"]), ("seq_0", "seq_1", "seq_2", "head")
    )
    return jax.shard_map(
        per_device,
        mesh=split,
        in_specs=(
            P(SEQ_HEAD, None),
            P(SEQ_HEAD, None),
            P(SEQ_HEAD, None),
            P(),
            P(),
            P(SEQ_HEAD),
            P(SEQ_HEAD),
        ),
        out_specs=(P(SEQ_HEAD, None), P(), P()),
        check_vma=False,
    )
```

profile of v0, /device:TPU:1, one launch (start us, length us, event | category | flops | bytes accessed | tf_op | source)
XLA Modules:
  0.0 200.0 jit_solution(16838395956209887631)
XLA Ops:
  0.6 2.8 %copy.36 = bf16[24,4,8,1024]{3,2,0,1:T(8,128)(2,1)} copy(bf16[24,4,8,1024]{3,2,1,0:T(8,128)(2,1)} %bitcast.54) | data formatting | bytes 3145728 | tf_op jit(solution)/shard_map/all_to_all | solution.py:68
  3.5 4.8 %all-to-all-start = ((bf16[192,4,1024]{2,0,1:T(8,128)(2,1)}), bf16[192,4,1024]{2,0,1:T(8,128)(2,1)S(1)}, u32[]{:S(2)}, u32[]{:S(2)}) async-start(bf16[192,4,1024]{2,0,1:T(8,128)(2,1)} %bitcast.40), calls=%async_computation | async-start | bytes 3145728 | tf_op jit(solution)/shard_map/all_to_all | solution.py:68
  8.3 1.3 copy.34
  9.6 17.5 %all-to-all-done = bf16[192,4,1024]{2,0,1:T(8,128)(2,1)S(1)} async-done(((bf16[192,4,1024]{2,0,1:T(8,128)(2,1)}), bf16[192,4,1024]{2,0,1:T(8,128)(2,1)S(1)}, u32[]{:S(2)}, u32[]{:S(2)}) %all-to-all-start) | async-done | bytes 1572896 | tf_op jit(solution)/shard_map/all_to_all | solution.py:68
  27.1 3.6 %all-to-all-start.2 = ((bf16[192,4,1024]{2,0,1:T(8,128)(2,1)}), bf16[192,4,1024]{2,0,1:T(8,128)(2,1)S(1)}, u32[]{:S(2)}, u32[]{:S(2)}) async-start(bf16[192,4,1024]{2,0,1:T(8,128)(2,1)} %bitcast.53), calls=%async_computation.2 | async-start | bytes 3145728 | tf_op jit(solution)/shard_map/all_to_all | solution.py:69
  30.7 6.1 %collective-permute-start = (bf16[768,1024]{1,0:T(8,128)(2,1)S(1)}, bf16[768,1024]{1,0:T(8,128)(2,1)}, u32[]{:S(2)}, u32[]{:S(2)}) collective-permute-start(bf16[768,1024]{1,0:T(8,128)(2,1)S(1)} %bitcast.44), channel_id=1, source_target_pairs={{0,4},{4,8},{8,12},{12,16},{16,20},{20,24},{24,28},{28,32},{32,36}... | collective-permute-start | bytes 4718600 | tf_op jit(solution)/shard_map/ppermute | solution.py:21
  36.8 1.2 slice.104
  38.0 1.9 collective-permute-start.1
  39.9 2.7 %copy.35 = bf16[24,4,8,1024]{3,2,0,1:T(8,128)(2,1)} copy(bf16[24,4,8,1024]{3,2,1,0:T(8,128)(2,1)} %bitcast.56) | data formatting | bytes 3145728 | tf_op jit(solution)/shard_map/all_to_all | solution.py:67
  42.6 6.0 %all-to-all-done.2 = bf16[192,4,1024]{2,0,1:T(8,128)(2,1)S(1)} async-done(((bf16[192,4,1024]{2,0,1:T(8,128)(2,1)}), bf16[192,4,1024]{2,0,1:T(8,128)(2,1)S(1)}, u32[]{:S(2)}, u32[]{:S(2)}) %all-to-all-start.2) | async-done | bytes 1572896 | tf_op jit(solution)/shard_map/all_to_all | solution.py:69
  48.5 4.3 %all-to-all-start.1 = ((bf16[192,4,1024]{2,0,1:T(8,128)(2,1)}), bf16[192,4,1024]{2,0,1:T(8,128)(2,1)}, u32[]{:S(2)}, u32[]{:S(2)}) async-start(bf16[192,4,1024]{2,0,1:T(8,128)(2,1)} %bitcast.51), calls=%async_computation.1 | async-start | bytes 3145728 | tf_op jit(solution)/shard_map/all_to_all | solution.py:67
  53.3 1.2 slice.107
  54.4 7.9 %collective-permute-start.2 = (bf16[768,1024]{1,0:T(8,128)(2,1)S(1)}, bf16[768,1024]{1,0:T(8,128)(2,1)}, u32[]{:S(2)}, u32[]{:S(2)}) collective-permute-start(bf16[768,1024]{1,0:T(8,128)(2,1)S(1)} %bitcast.42), channel_id=1, source_target_pairs={{0,4},{4,8},{8,12},{12,16},{16,20},{20,24},{24,28},{28,32},{32,36}... | collective-permute-start | bytes 4718600 | tf_op jit(solution)/shard_map/ppermute | solution.py:21
  62.3 1.9 collective-permute-start.3
  64.2 3.7 %pad_maximum_fusion = bf16[2176,1024]{1,0:T(8,128)(2,1)} fusion(bf16[640,1024]{1,0:T(8,128)(2,1)} %collective-permute-done.1, bf16[768,1024]{1,0:T(8,128)(2,1)S(1)} %bitcast.46, bf16[768,1024]{1,0:T(8,128)(2,1)} %collective-permute-done), kind=kLoop, calls=%fused_computation.33 | loop fusion | flops 13369344 | bytes 8912896 | tf_op jit(solution)/shard_map/concatenate | solution.py:84
  67.9 1.7 all-to-all-done.1
  69.6 4.2 %fusion.138 = (f32[768]{0:T(1024)S(1)}, f32[768,2176]{0,1:T(8,128)S(1)}) fusion(bf16[768,1024]{1,0:T(8,128)(2,1)} %bitcast.4, bf16[2176,1024]{1,0:T(8,128)(2,1)} %pad_maximum_fusion, pred[2176]{0:T(1024)(128)(4,1)S(1)} %fusion.137, pred[768]{0:T(1024)(128)(4,1)S(1)} %dynamic-slice_compare_fusion, s32[768]{0:T(1024)S(1)} %iota_add_fusion.1, ...), kind=kOutput, calls=%fused_computation.114 | convolution fusion | flops 441187584 | bytes 7467904 | tf_op jit(solution)/shard_map/dot_general | solution.py:48
  73.9 6.3 %fusion.139 = (f32[768]{0:T(1024)S(1)}, f32[768,2176]{0,1:T(8,128)}) fusion(bf16[768,1024]{1,0:T(8,128)(2,1)} %bitcast.4, bf16[2176,1024]{1,0:T(8,128)(2,1)S(1)} %copy-done.1, pred[2176]{0:T(1024)(128)(4,1)S(1)} %fusion.137, pred[768]{0:T(1024)(128)(4,1)S(1)} %dynamic-slice_compare_fusion, s32[768]{0:T(1024)S(1)} %iota_add_fusion.1, ...), kind=kOutput, calls=%fused_computation.115 | convolution fusion | flops 441187584 | bytes 7478272 | tf_op jit(solution)/shard_map/dot_general | solution.py:48
  80.1 5.9 %fusion.140 = (f32[768]{0:T(1024)S(1)}, f32[768,2176]{0,1:T(8,128)}) fusion(bf16[768,1024]{1,0:T(8,128)(2,1)} %bitcast.4, bf16[2176,1024]{1,0:T(8,128)(2,1)S(1)} %copy-done.1, pred[2176]{0:T(1024)(128)(4,1)S(1)} %fusion.137, pred[768]{0:T(1024)(128)(4,1)S(1)} %dynamic-slice_compare_fusion, s32[768]{0:T(1024)S(1)} %iota_add_fusion.1, ...), kind=kOutput, calls=%fused_computation.116 | convolution fusion | flops 441187584 | bytes 7478272 | tf_op jit(solution)/shard_map/dot_general | solution.py:48
  86.0 6.0 %fusion.141 = (f32[768]{0:T(1024)S(1)}, f32[768,2176]{0,1:T(8,128)}) fusion(bf16[768,1024]{1,0:T(8,128)(2,1)} %bitcast.4, bf16[2176,1024]{1,0:T(8,128)(2,1)S(1)} %copy-done.1, pred[2176]{0:T(1024)(128)(4,1)S(1)} %fusion.137, pred[768]{0:T(1024)(128)(4,1)S(1)} %dynamic-slice_compare_fusion, s32[768]{0:T(1024)S(1)} %iota_add_fusion.1, ...), kind=kOutput, calls=%fused_computation.117 | convolution fusion | flops 441187584 | bytes 7478272 | tf_op jit(solution)/shard_map/dot_general | solution.py:48
  92.0 3.6 %fusion.142 = (f32[768]{0:T(1024)S(1)}, f32[768,2176]{0,1:T(8,128)S(1)}) fusion(bf16[768,1024]{1,0:T(8,128)(2,1)} %bitcast.4, bf16[2176,1024]{1,0:T(8,128)(2,1)S(1)} %copy-done.1, pred[2176]{0:T(1024)(128)(4,1)S(1)} %fusion.137, pred[768]{0:T(1024)(128)(4,1)S(1)} %dynamic-slice_compare_fusion, s32[768]{0:T(1024)S(1)} %iota_add_fusion.1, ...), kind=kOutput, calls=%fused_computation.118 | convolution fusion | flops 441187584 | bytes 7478272 | tf_op jit(solution)/shard_map/dot_general | solution.py:48
  95.7 3.6 %fusion.143 = (f32[768]{0:T(1024)S(1)}, f32[768,2176]{0,1:T(8,128)S(1)}) fusion(bf16[768,1024]{1,0:T(8,128)(2,1)} %bitcast.4, bf16[2176,1024]{1,0:T(8,128)(2,1)S(1)} %copy-done.1, pred[2176]{0:T(1024)(128)(4,1)S(1)} %fusion.137, pred[768]{0:T(1024)(128)(4,1)S(1)} %dynamic-slice_compare_fusion, s32[768]{0:T(1024)S(1)} %iota_add_fusion.1, ...), kind=kOutput, calls=%fused_computation.119 | convolution fusion | flops 441187584 | bytes 7478272 | tf_op jit(solution)/shard_map/dot_general | solution.py:48
  99.3 1.0 fusion
  100.3 3.6 %fusion.144 = (f32[768]{0:T(1024)S(1)}, f32[768,2176]{0,1:T(8,128)S(1)}) fusion(bf16[768,1024]{1,0:T(8,128)(2,1)} %bitcast.4, bf16[2176,1024]{1,0:T(8,128)(2,1)S(1)} %copy-done.1, pred[2176]{0:T(1024)(128)(4,1)S(1)} %fusion.137, pred[768]{0:T(1024)(128)(4,1)S(1)} %dynamic-slice_compare_fusion, s32[768]{0:T(1024)S(1)} %iota_add_fusion.1, ...), kind=kOutput, calls=%fused_computation.120 | convolution fusion | flops 441187584 | bytes 7478272 | tf_op jit(solution)/shard_map/dot_general | solution.py:48
  103.9 3.9 %fusion.145 = (f32[768]{0:T(1024)S(1)}, f32[768,2176]{0,1:T(8,128)S(1)}) fusion(bf16[768,1024]{1,0:T(8,128)(2,1)} %bitcast.4, bf16[2176,1024]{1,0:T(8,128)(2,1)S(1)} %copy-done.1, pred[2176]{0:T(1024)(128)(4,1)S(1)} %fusion.137, pred[768]{0:T(1024)(128)(4,1)S(1)} %dynamic-slice_compare_fusion, s32[768]{0:T(1024)S(1)} %iota_add_fusion.1, ...), kind=kOutput, calls=%fused_computation.121 | convolution fusion | flops 441187584 | bytes 7478272 | tf_op jit(solution)/shard_map/dot_general | solution.py:48
  107.8 3.9 %pad_maximum_fusion.1 = bf16[2176,1024]{1,0:T(8,128)(2,1)} fusion(bf16[640,1024]{1,0:T(8,128)(2,1)} %collective-permute-done.3, bf16[768,1024]{1,0:T(8,128)(2,1)S(1)} %bitcast.43, bf16[768,1024]{1,0:T(8,128)(2,1)} %collective-permute-done.2), kind=kLoop, calls=%fused_computation.34 | loop fusion | flops 13369344 | bytes 8912896 | tf_op jit(solution)/shard_map/concatenate | solution.py:87
  111.7 4.3 %fusion.46 = bf16[768,1024]{0,1:T(8,128)(2,1)S(1)} fusion(f32[768,2176]{0,1:T(8,128)} %copy-done, f32[768]{0:T(1024)S(1)} %get-tuple-element.13, bf16[2176,1024]{1,0:T(8,128)(2,1)} %pad_maximum_fusion.1, f32[768]{0:T(1024)S(1)} %fusion), kind=kOutput, calls=%fused_computation.56 | convolution fusion | flops 431357952 | bytes 7444480 | tf_op jit(solution)/shard_map/dot_general | solution.py:58
  116.0 1.0 fusion.2
  117.0 2.3 %fusion.55 = bf16[768,1024]{0,1:T(8,128)(2,1)S(1)} fusion(bf16[768,1024]{0,1:T(8,128)(2,1)S(1)} %fusion.46, f32[768,2176]{0,1:T(8,128)S(1)} %bitcast.50, f32[768]{0:T(1024)S(1)} %get-tuple-element.15, bf16[2176,1024]{1,0:T(8,128)(2,1)} %pad_maximum_fusion.1, f32[768]{0:T(1024)S(1)} %fusion.2), kind=kOutput, calls=%fused_computation.59 | convolution fusion | flops 431357952 | bytes 7446528 | tf_op jit(solution)/shard_map/dot_general | solution.py:58
  119.3 4.0 %fusion.4 = f32[768]{0:T(1024)S(1)} fusion(f32[768,2176]{0,1:T(8,128)} %get-tuple-element.18, f32[768]{0:T(1024)S(1)} %get-tuple-element.17), kind=kLoop, calls=%fused_computation.21 | loop fusion | flops 3341568 | bytes 6690816 | tf_op jit(solution)/shard_map/reduce_sum | solution.py:56
  123.2 4.3 %fusion.64 = bf16[768,1024]{0,1:T(8,128)(2,1)S(1)} fusion(bf16[768,1024]{0,1:T(8,128)(2,1)S(1)} %fusion.55, f32[768,2176]{0,1:T(8,128)} %get-tuple-element.18, f32[768]{0:T(1024)S(1)} %get-tuple-element.17, bf16[2176,1024]{1,0:T(8,128)(2,1)} %pad_maximum_fusion.1, f32[768]{0:T(1024)S(1)} %fusion.4), kind=kOutput, calls=%fused_computation.62 | convolution fusion | flops 431357952 | bytes 7446528 | tf_op jit(solution)/shard_map/dot_general | solution.py:58
  127.6 1.0 fusion.6
  128.5 2.3 %fusion.73 = bf16[768,1024]{0,1:T(8,128)(2,1)S(1)} fusion(bf16[768,1024]{0,1:T(8,128)(2,1)S(1)} %fusion.64, f32[768,2176]{0,1:T(8,128)S(1)} %bitcast.48, f32[768]{0:T(1024)S(1)} %get-tuple-element.19, bf16[2176,1024]{1,0:T(8,128)(2,1)} %pad_maximum_fusion.1, f32[768]{0:T(1024)S(1)} %fusion.6), kind=kOutput, calls=%fused_computation.65 | convolution fusion | flops 431357952 | bytes 7446528 | tf_op jit(solution)/shard_map/dot_general | solution.py:58
  130.8 1.0 fusion.8
  131.8 2.3 %fusion.82 = bf16[768,1024]{0,1:T(8,128)(2,1)S(1)} fusion(bf16[768,1024]{0,1:T(8,128)(2,1)S(1)} %fusion.73, f32[768,2176]{0,1:T(8,128)S(1)} %get-tuple-element.22, f32[768]{0:T(1024)S(1)} %get-tuple-element.21, bf16[2176,1024]{1,0:T(8,128)(2,1)} %pad_maximum_fusion.1, f32[768]{0:T(1024)S(1)} %fusion.8), kind=kOutput, calls=%fused_computation.68 | convolution fusion | flops 431357952 | bytes 7446528 | tf_op jit(solution)/shard_map/dot_general | solution.py:58
  134.0 1.0 fusion.10
  135.0 2.3 %fusion.91 = bf16[768,1024]{0,1:T(8,128)(2,1)S(1)} fusion(bf16[768,1024]{0,1:T(8,128)(2,1)S(1)} %fusion.82, f32[768,2176]{0,1:T(8,128)S(1)} %get-tuple-element.24, f32[768]{0:T(1024)S(1)} %get-tuple-element.23, bf16[2176,1024]{1,0:T(8,128)(2,1)} %pad_maximum_fusion.1, f32[768]{0:T(1024)S(1)} %fusion.10), kind=kOutput, calls=%fused_computation.71 | convolution fusion | flops 431357952 | bytes 7446528 | tf_op jit(solution)/shard_map/dot_general | solution.py:58
  137.3 1.2 fusion.12
  138.5 2.3 %fusion.100 = bf16[768,1024]{0,1:T(8,128)(2,1)S(1)} fusion(bf16[768,1024]{0,1:T(8,128)(2,1)S(1)} %fusion.91, f32[768,2176]{0,1:T(8,128)S(1)} %get-tuple-element.26, f32[768]{0:T(1024)S(1)} %get-tuple-element.25, bf16[2176,1024]{1,0:T(8,128)(2,1)} %pad_maximum_fusion.1, f32[768]{0:T(1024)S(1)} %fusion.12), kind=kOutput, calls=%fused_computation.74 | convolution fusion | flops 431357952 | bytes 7446528 | tf_op jit(solution)/shard_map/dot_general | solution.py:58
  140.7 1.0 fusion.14
  141.7 2.3 %fusion.109 = bf16[768,1024]{0,1:T(8,128)(2,1)S(1)} fusion(bf16[768,1024]{0,1:T(8,128)(2,1)S(1)} %fusion.100, f32[768,2176]{0,1:T(8,128)S(1)} %get-tuple-element.28, f32[768]{0:T(1024)S(1)} %get-tuple-element.27, bf16[2176,1024]{1,0:T(8,128)(2,1)} %pad_maximum_fusion.1, f32[768]{0:T(1024)S(1)} %fusion.14), kind=kOutput, calls=%fused_computation.77 | convolution fusion | flops 431357952 | bytes 7446528 | tf_op jit(solution)/shard_map/dot_general | solution.py:58
  144.0 1.6 copy.25
  145.6 3.6 %all-to-all-start.3 = ((bf16[4,192,1024]{2,1,0:T(8,128)(2,1)}), bf16[4,192,1024]{2,1,0:T(8,128)(2,1)S(1)}, u32[]{:S(2)}, u32[]{:S(2)}) async-start(bf16[4,192,1024]{2,1,0:T(8,128)(2,1)} %bitcast.17), calls=%async_computation.3 | async-start | bytes 3145728 | tf_op jit(solution)/shard_map/all_to_all | solution.py:109
  149.4 20.6 %all-reduce.2 = (f32[128]{0:T(128)S(1)}, f32[128]{0:T(128)S(1)}) all-reduce(f32[128]{0:T(128)S(1)} %get-tuple-element.4, f32[128]{0:T(128)S(1)} %get-tuple-element.3), channel_id=1, replica_groups=mesh['seq_0'=8,'seq_1'=4,'seq_2'=2,'head'=4] {'seq_0'}, use_global_device_ids=true, to_apply=%region_17.18 | all-reduce | flops 256 | bytes 2048 | tf_op jit(solution)/shard_map/psum | solution.py:25
  170.1 8.5 %all-reduce.4 = (f32[128]{0:T(128)S(1)}, f32[128]{0:T(128)S(1)}) all-reduce(f32[128]{0:T(128)S(1)} %get-tuple-element.5, f32[128]{0:T(128)S(1)} %get-tuple-element.6), channel_id=1, replica_groups=mesh['seq_0'=8,'seq_1'=4,'seq_2'=2,'head'=4] {'seq_1'}, use_global_device_ids=true, to_apply=%region_18.19 | all-reduce | flops 256 | bytes 2048 | tf_op jit(solution)/shard_map/psum | solution.py:25
  178.6 10.7 %all-reduce.5 = (f32[128]{0:T(128)S(1)}, f32[128]{0:T(128)S(1)}) all-reduce(f32[128]{0:T(128)S(1)} %get-tuple-element.9, f32[128]{0:T(128)S(1)} %get-tuple-element.10), channel_id=1, replica_groups=mesh['seq_0'=8,'seq_1'=4,'seq_2'=2,'head'=4] {'seq_2'}, use_global_device_ids=true, to_apply=%region_19.20 | all-reduce | flops 256 | bytes 2048 | tf_op jit(solution)/shard_map/psum | solution.py:25
  189.3 8.9 %all-reduce.3 = (f32[128]{0:T(128)S(1)}, f32[128]{0:T(128)S(1)}) all-reduce(f32[128]{0:T(128)S(1)} %get-tuple-element.11, f32[128]{0:T(128)S(1)} %get-tuple-element.12), channel_id=1, replica_groups=mesh['seq_0'=8,'seq_1'=4,'seq_2'=2,'head'=4] {'head'}, use_global_device_ids=true, to_apply=%region_20.21 | all-reduce | flops 256 | bytes 2048 | tf_op jit(solution)/shard_map/psum | solution.py:25
  198.7 1.3 copy.30
  (41 shorter events, 1.2 us)
Async XLA Ops:
  0.6 7.7 %copy-start.2 = (bf16[192,4096]{1,0:T(8,128)(2,1)S(1)}, bf16[192,4096]{1,0:T(8,128)(2,1)}, u32[]{:S(2)}) copy-start(bf16[192,4096]{1,0:T(8,128)(2,1)} %param.9) | copy-start | bytes 4718596
  3.5 23.7 %all-to-all-start = ((bf16[192,4,1024]{2,0,1:T(8,128)(2,1)}), bf16[192,4,1024]{2,0,1:T(8,128)(2,1)S(1)}, u32[]{:S(2)}, u32[]{:S(2)}) async-start(bf16[192,4,1024]{2,0,1:T(8,128)(2,1)} %bitcast.40), calls=%async_computation | async-start | bytes 3145728 | tf_op jit(solution)/shard_map/all_to_all | solution.py:68
  27.1 21.4 %all-to-all-start.2 = ((bf16[192,4,1024]{2,0,1:T(8,128)(2,1)}), bf16[192,4,1024]{2,0,1:T(8,128)(2,1)S(1)}, u32[]{:S(2)}, u32[]{:S(2)}) async-start(bf16[192,4,1024]{2,0,1:T(8,128)(2,1)} %bitcast.53), calls=%async_computation.2 | async-start | bytes 3145728 | tf_op jit(solution)/shard_map/all_to_all | solution.py:69
  30.7 22.2 %copy-start.3 = (s32[49152]{0:T(1024)S(1)}, s32[49152]{0:T(1024)}, u32[]{:S(2)}) copy-start(s32[49152]{0:T(1024)} %param.10) | copy-start | bytes 589828
  30.7 22.3 %copy-start.4 = (s32[49152]{0:T(1024)S(1)}, s32[49152]{0:T(1024)}, u32[]{:S(2)}) copy-start(s32[49152]{0:T(1024)} %param.11) | copy-start | bytes 589828
  30.7 33.5 %collective-permute-start = (bf16[768,1024]{1,0:T(8,128)(2,1)S(1)}, bf16[768,1024]{1,0:T(8,128)(2,1)}, u32[]{:S(2)}, u32[]{:S(2)}) collective-permute-start(bf16[768,1024]{1,0:T(8,128)(2,1)S(1)} %bitcast.44), channel_id=1, source_target_pairs={{0,4},{4,8},{8,12},{12,16},{16,20},{20,24},{24,28},{28,32},{32,36}... | collective-permute-start | bytes 4718600 | tf_op jit(solution)/shard_map/ppermute | solution.py:21
  38.0 26.3 %collective-permute-start.1 = (bf16[640,1024]{1,0:T(8,128)(2,1)}, bf16[640,1024]{1,0:T(8,128)(2,1)}, u32[]{:S(2)}, u32[]{:S(2)}) collective-permute-start(bf16[640,1024]{1,0:T(8,128)(2,1)} %slice.104), channel_id=1, source_target_pairs={{4,0},{8,4},{12,8},{16,12},{20,16},{24,20},{28,24},{32,28},{36,32}... | collective-permute-start | bytes 3932168 | tf_op jit(solution)/shard_map/ppermute | solution.py:21
  48.5 21.1 %all-to-all-start.1 = ((bf16[192,4,1024]{2,0,1:T(8,128)(2,1)}), bf16[192,4,1024]{2,0,1:T(8,128)(2,1)}, u32[]{:S(2)}, u32[]{:S(2)}) async-start(bf16[192,4,1024]{2,0,1:T(8,128)(2,1)} %bitcast.51), calls=%async_computation.1 | async-start | bytes 3145728 | tf_op jit(solution)/shard_map/all_to_all | solution.py:67
  54.4 53.4 %collective-permute-start.2 = (bf16[768,1024]{1,0:T(8,128)(2,1)S(1)}, bf16[768,1024]{1,0:T(8,128)(2,1)}, u32[]{:S(2)}, u32[]{:S(2)}) collective-permute-start(bf16[768,1024]{1,0:T(8,128)(2,1)S(1)} %bitcast.42), channel_id=1, source_target_pairs={{0,4},{4,8},{8,12},{12,16},{16,20},{20,24},{24,28},{28,32},{32,36}... | collective-permute-start | bytes 4718600 | tf_op jit(solution)/shard_map/ppermute | solution.py:21
  62.3 45.5 %collective-permute-start.3 = (bf16[640,1024]{1,0:T(8,128)(2,1)}, bf16[640,1024]{1,0:T(8,128)(2,1)}, u32[]{:S(2)}, u32[]{:S(2)}) collective-permute-start(bf16[640,1024]{1,0:T(8,128)(2,1)} %slice.107), channel_id=1, source_target_pairs={{4,0},{8,4},{12,8},{16,12},{20,16},{24,20},{28,24},{32,28},{36,32}... | collective-permute-start | bytes 3932168 | tf_op jit(solution)/shard_map/ppermute | solution.py:21
  69.6 4.2 %copy-start.1 = (bf16[2176,1024]{1,0:T(8,128)(2,1)S(1)}, bf16[2176,1024]{1,0:T(8,128)(2,1)}, u32[]{:S(2)}) copy-start(bf16[2176,1024]{1,0:T(8,128)(2,1)} %pad_maximum_fusion) | copy-start | bytes 13369348
  73.8 25.5 %copy-start = (f32[768,2176]{0,1:T(8,128)}, f32[768,2176]{0,1:T(8,128)S(1)}, u32[]{:S(2)}) copy-start(f32[768,2176]{0,1:T(8,128)S(1)} %get-tuple-element.14) | copy-start | bytes 20054020
  107.8 8.2 %slice-start.2 = ((s8[6684672]{0:T(1024)(128)(4,1)}), s8[4194304]{0:T(1024)(128)(4,1)S(1)}, s32[]{:S(2)}) async-start(s8[6684672]{0:T(1024)(128)(4,1)} %bitcast.49), calls=%async_computation.6 | async-start | bytes 8388608
  111.7 4.3 %slice-start.3 = ((s8[6684672]{0:T(1024)(128)(4,1)}), s8[2490368]{0:T(1024)(128)(4,1)S(1)}, s32[]{:S(2)}) async-start(s8[6684672]{0:T(1024)(128)(4,1)} %bitcast.49), calls=%async_computation.7 | async-start | bytes 4980736
  119.2 8.3 %slice-start = ((s8[6684672]{0:T(1024)(128)(4,1)}), s8[4194304]{0:T(1024)(128)(4,1)S(1)}, s32[]{:S(2)}) async-start(s8[6684672]{0:T(1024)(128)(4,1)} %bitcast.47), calls=%async_computation.4 | async-start | bytes 8388608
  123.2 4.3 %slice-start.1 = ((s8[6684672]{0:T(1024)(128)(4,1)}), s8[2490368]{0:T(1024)(128)(4,1)S(1)}, s32[]{:S(2)}) async-start(s8[6684672]{0:T(1024)(128)(4,1)} %bitcast.47), calls=%async_computation.5 | async-start | bytes 4980736
  144.0 5.3 %copy-start.6 = (s32[192]{0:T(256)S(1)}, s32[192]{0:T(256)}, u32[]{:S(2)}) copy-start(s32[192]{0:T(256)} %param.12) | copy-start | bytes 2308
  144.0 5.3 %copy-start.5 = (f32[192]{0:T(256)S(1)}, f32[192]{0:T(256)}, u32[]{:S(2)}) copy-start(f32[192]{0:T(256)} %param.13) | copy-start | bytes 2308
  145.6 53.0 %all-to-all-start.3 = ((bf16[4,192,1024]{2,1,0:T(8,128)(2,1)}), bf16[4,192,1024]{2,1,0:T(8,128)(2,1)S(1)}, u32[]{:S(2)}, u32[]{:S(2)}) async-start(bf16[4,192,1024]{2,1,0:T(8,128)(2,1)} %bitcast.17), calls=%async_computation.3 | async-start | bytes 3145728 | tf_op jit(solution)/shard_map/all_to_all | solution.py:109
  198.1 1.8 copy-start.7
where the time goes:
time: 201 us; the launch traced here: 200 us
  matrix products  59.3 us (30%)
  blocking collectives  48.7 us (24%)
  starting transfers between devices  34.1 us (17%)
  waiting for transfers between devices  25.2 us (13%)
  other arithmetic  19.3 us (10%)
  local copies, waits for them, and re-layouts  12.4 us (6%)
    psum x4, blocking collectives, over_axes(): return functools.reduce(lax.psum, axes, value)  48.7 us
    dot_general x8, matrix products, attend(): lax.dot_general(query_head, key_head, (((1,), (1,)), ((), ())), preferred...  37.1 us
    dot_general x8, matrix products, attend(): jnp.dot(weights.astype(jnp.bfloat16), value_head, preferred_element_type=...  22.2 us
    ppermute x4, starting transfers between devices, shifted(): return lax.ppermute(block, axis, route)  17.8 us
    all_to_all x1, waiting for transfers between devices, per_device(): lax.all_to_all(key_rows, 'head', split_axis=1, concat_axis=0, tiled=True)  17.5 us
    reduce_sum x8, other arithmetic, attend(): total = jnp.sum(weights, axis=1, keepdims=True)  10.9 us
    all_to_all x1, waiting for transfers between devices, per_device(): lax.all_to_all(values, 'head', split_axis=1, concat_axis=0, tiled=True)  5.95 us
    all_to_all x1, starting transfers between devices, per_device(): lax.all_to_all(key_rows, 'head', split_axis=1, concat_axis=0, tiled=True)  4.84 us
  transfers between devices with their start and end apart: 8, of which 3 were waited for; matrix products, arithmetic and copies ran while one was open for 25% of the time, Pallas kernels for 0%

commit v1 on v0

v1 whole, which is shorter than its diff:
```python
import functools
import math

import jax
import jax.numpy as jnp
from jax import lax
from jax.experimental import pallas as pl
from jax.experimental.pallas import tpu as pltpu
from jax.sharding import Mesh
from jax.sharding import PartitionSpec as P

HEAD_DIM = 128
DOC_MEAN = 384
NZ, NY, NC, NX = 8, 4, 2, 4
GROUP = NC * NX
STRIP = 192
BLOCK = STRIP * GROUP
BLOCKS = NZ * NY
HEADS = 4
BACK, AHEAD = 704, 576
FRONT = 768
SPAN = 1536
WINDOW = FRONT + BLOCK + 640
DEPTH = 3
LANES = 128
AXES = ("z", "y", "c", "x")
MESH = pl.DeviceIdType.MESH


def first_key(strip):
    return pl.multiple_of(((3 * strip + 1) // 2) * LANES, LANES)


def kernel(
    q_hbm,
    k_hbm,
    v_hbm,
    docs_hbm,
    flags_hbm,
    stat_ref,
    out_hbm,
    count_ref,
    loss_ref,
    q_buf,
    k_buf,
    v_buf,
    o_buf,
    bias,
    docs,
    flags,
    q_docs,
    q_images,
    slots_a,
    slots_b,
    slots_c,
    id_sem,
    in_send,
    in_recv,
    halo_send,
    halo_recv,
    out_send,
    out_recv,
    stat_send,
    stat_recv,
):
    z, y, c, x = (lax.axis_index(name) for name in AXES)
    me = c * NX + x
    block = z * NY + y
    after = lax.rem(block + 1, BLOCKS)
    before = lax.rem(block + BLOCKS - 1, BLOCKS)

    def member(index):
        return {"z": z, "y": y, "c": lax.div(index, NX), "x": lax.rem(index, NX)}

    def in_block(index):
        return {"z": lax.div(index, NY), "y": lax.rem(index, NY), "c": c, "x": x}

    def along_y(index):
        return {"z": z, "y": index, "c": c, "x": x}

    def along_z(index):
        return {"z": index, "y": y, "c": c, "x": x}

    id_copies = [
        pltpu.make_async_copy(docs_hbm, docs, id_sem.at[0]),
        pltpu.make_async_copy(flags_hbm, flags, id_sem.at[1]),
    ]
    for copy in id_copies:
        copy.start()

    barrier = pltpu.get_barrier_semaphore()
    peers = [member(lax.rem(me + o, GROUP)) for o in range(1, GROUP)]
    peers += [in_block(after), in_block(before)]
    peers += [along_y(lax.rem(y + o, NY)) for o in range(1, NY)]
    peers += [along_z(lax.rem(z + o, NZ)) for o in range(1, NZ)]
    for peer in peers:
        pl.semaphore_signal(barrier, inc=1, device_id=peer, device_id_type=MESH)
    pl.semaphore_wait(barrier, len(peers))

    sources = (k_hbm, v_hbm, q_hbm)
    targets = (k_buf, v_buf, q_buf)
    bases = (FRONT, FRONT, 0)

    def piece(array, head, owner):
        columns = pl.ds(pl.multiple_of(owner * HEADS * HEAD_DIM + head * HEAD_DIM, LANES), HEAD_DIM)
        rows = pl.ds(pl.multiple_of(bases[array] + me * STRIP, 64), STRIP)
        return sources[array].at[:, columns], targets[array].at[head, rows, :]

    def start_group(group):
        array, head = divmod(group, HEADS)

        def send(o, carry):
            owner = lax.rem(me + o, GROUP)
            source, target = piece(array, head, owner)
            pltpu.make_async_remote_copy(
                src_ref=source,
                dst_ref=target,
                send_sem=in_send.at[array],
                recv_sem=in_recv.at[array, head],
                device_id=member(owner),
                device_id_type=MESH,
            ).start()
            return carry

        lax.fori_loop(1, GROUP, send, 0)
        source, target = piece(array, head, me)
        pltpu.make_async_copy(source, target, in_recv.at[array, head]).start()

    def wait_group(group):
        array, head = divmod(group, HEADS)
        rows = targets[array].at[head, pl.ds(bases[array], BLOCK), :]
        pltpu.make_async_copy(rows, rows, in_recv.at[array, head]).wait()

    def start_halo(array, head):
        buffer = targets[array]
        for rows, first, target, peer in (
            (BACK, FRONT + BLOCK - BACK, FRONT - BACK, after),
            (AHEAD, FRONT, FRONT + BLOCK, before),
        ):
            pltpu.make_async_remote_copy(
                src_ref=buffer.at[head, pl.ds(first, rows), :],
                dst_ref=buffer.at[head, pl.ds(target, rows), :],
                send_sem=halo_send.at[array],
                recv_sem=halo_recv.at[array, head],
                device_id=in_block(peer),
                device_id_type=MESH,
            ).start()

    def stage_send(number, slots, own, size, peer_of):
        def send(o, carry):
            pltpu.make_async_remote_copy(
                src_ref=slots.at[own],
                dst_ref=slots.at[own],
                send_sem=stat_send.at[number],
                recv_sem=stat_recv.at[number],
                device_id=peer_of(lax.rem(own + o, size)),
                device_id_type=MESH,
            ).start()
            return carry

        lax.fori_loop(1, size, send, 0)

    def stage_sum(number, slots, size):
        others = slots.at[pl.ds(0, size - 1)]
        pltpu.make_async_copy(others, others, stat_recv.at[number]).wait()
        total = slots[0]
        for i in range(1, size):
            total = total + slots[i]
        return total

    def after_groups(group):
        if group == 0:
            for copy in id_copies:
                copy.wait()
            make_query_ids()
        elif group == 1:
            total = stage_sum(0, slots_a, GROUP)
            slots_b[y] = total
            stage_send(1, slots_b, y, NY, along_y)
        elif group == 3:
            total = stage_sum(1, slots_b, NY)
            slots_c[z] = total
            stage_send(2, slots_c, z, NZ, along_z)
        elif group == 5:
            total = stage_sum(2, slots_c, NZ)
            counts = total[0:1]
            count_ref[...] = counts
            loss_ref[...] = total[1:2] / jnp.maximum(counts, 1.0)

    def id_row(row):
        at = pl.ds(lax.rem(block * (BLOCK // LANES) + row + BLOCKS * (BLOCK // LANES), BLOCKS * (BLOCK // LANES)), 1)
        doc = docs[at, :]
        return doc, jnp.where(flags[at, :] == 1, doc, -1)

    def make_query_ids():
        def one(row, carry):
            at = pl.ds(pl.multiple_of(row * LANES, LANES), LANES)
            doc, image = id_row(row)
            q_docs[at, :] = jnp.broadcast_to(doc, (LANES, LANES)).T
            q_images[at, :] = jnp.broadcast_to(image, (LANES, LANES)).T
            return carry

        lax.fori_loop(0, BLOCK // LANES, one, 0)

    def make_bias(strip):
        start = first_key(strip)
        rows = pl.ds(pl.multiple_of(strip * STRIP, 64), STRIP)
        doc, image = q_docs[rows, :], q_images[rows, :]
        shape = (STRIP, LANES)
        offset = lax.broadcasted_iota(jnp.int32, shape, 1) - lax.broadcasted_iota(jnp.int32, shape, 0)
        first_row = lax.div(start, LANES) - FRONT // LANES
        for i in range(SPAN // LANES):
            key_doc, key_image = id_row(first_row + i)
            key_image = jnp.where(key_image < 0, -2, key_image)
            earlier = offset <= FRONT + strip * STRIP - start - i * LANES
            allowed = ((doc == key_doc) & earlier) | (image == key_image)
            bias[rows, i * LANES : (i + 1) * LANES] = jnp.where(allowed, 0.0, -jnp.inf)

    def attend(head, strip):
        start = first_key(strip)
        rows = pl.ds(pl.multiple_of(strip * STRIP, 64), STRIP)
        keys = pl.ds(start, SPAN)
        scores = lax.dot_general(
            q_buf[head, rows, :],
            k_buf[head, keys, :],
            (((1,), (1,)), ((), ())),
            preferred_element_type=jnp.float32,
        )
        scores = scores * (HEAD_DIM**-0.5 * math.log2(math.e)) + bias[rows, :]
        weights = jnp.exp2(scores - jnp.max(scores, axis=1, keepdims=True))
        total = jnp.sum(weights, axis=1, keepdims=True)
        mixed = jnp.dot(
            weights.astype(jnp.bfloat16), v_buf[head, keys, :], preferred_element_type=jnp.float32
        )
        o_buf[head, rows, :] = (mixed / total).astype(jnp.bfloat16)
        columns = pl.ds(pl.multiple_of(me * HEADS * HEAD_DIM + head * HEAD_DIM, LANES), HEAD_DIM)
        source, target = o_buf.at[head, rows, :], out_hbm.at[:, columns]

        @pl.when(strip == me)
        def _():
            pltpu.make_async_copy(source, target, out_recv).start()

        @pl.when(strip != me)
        def _():
            pltpu.make_async_remote_copy(
                src_ref=source,
                dst_ref=target,
                send_sem=out_send,
                recv_sem=out_recv,
                device_id=member(strip),
                device_id_type=MESH,
            ).start()

    for group in range(DEPTH):
        start_group(group)
    slots_a[me] = stat_ref[...]
    stage_send(0, slots_a, me, GROUP, member)

    edge = jnp.zeros((HEADS, 64, HEAD_DIM), jnp.bfloat16)
    for buffer in (k_buf, v_buf):
        buffer[:, 0 : FRONT - BACK, :] = edge
        buffer[:, FRONT + BLOCK + AHEAD : WINDOW, :] = edge

    for group in range(2 * HEADS):
        wait_group(group)
        start_halo(*divmod(group, HEADS))
        start_group(group + DEPTH)
        after_groups(group)
        make_bias(group)

    for head in range(HEADS):
        for array in range(2):
            rows = targets[array].at[head, pl.ds(0, BACK + AHEAD), :]
            pltpu.make_async_copy(rows, rows, halo_recv.at[array, head]).wait()
        group = 2 * HEADS + head
        wait_group(group)
        if group + DEPTH < 3 * HEADS:
            start_group(group + DEPTH)

        def step(i, carry, head=head):
            attend(head, lax.rem(me + i, GROUP))
            return carry

        lax.fori_loop(1, GROUP + 1, step, 0)

    def drain(ref, sem):
        pltpu.make_async_copy(ref, ref, sem).wait()

    for array in range(3):
        drain(targets[array].at[:, pl.ds(0, BLOCK - STRIP), :], in_send.at[array])
    for array in range(2):
        drain(targets[array].at[:, pl.ds(0, BACK + AHEAD), :], halo_send.at[array])
    for number, slots, size in ((0, slots_a, GROUP), (1, slots_b, NY), (2, slots_c, NZ)):
        drain(slots.at[pl.ds(0, size - 1)], stat_send.at[number])
    drain(o_buf.at[:, pl.ds(0, BLOCK - STRIP), :], out_send)
    drain(out_hbm, out_recv)


def per_device(queries, key_rows, values, doc_ids, image_flags, labels, token_loss):
    rows = labels.shape[0]
    place = ((lax.axis_index("z") * NY + lax.axis_index("y")) * NC + lax.axis_index("c")) * NX + lax.axis_index("x")
    local_docs = lax.dynamic_slice_in_dim(doc_ids, place * rows, rows)
    documents = doc_ids.shape[0] // DOC_MEAN
    member = (local_docs[:, None] == jnp.arange(documents, dtype=jnp.int32)[None, :]) & (labels[:, None] >= 0)
    counts = jnp.sum(member.astype(jnp.float32), axis=0)
    sums = jnp.sum(jnp.where(member, token_loss[:, None], jnp.float32(0.0)), axis=0)
    stats = jnp.pad(jnp.stack([counts, sums]), ((0, 6), (0, 0)))
    id_shape = (BLOCKS * BLOCK // LANES, LANES)
    anywhere = pl.BlockSpec(memory_space=pl.ANY)
    local = pl.BlockSpec(memory_space=pltpu.VMEM)
    window = pltpu.VMEM((HEADS, WINDOW, HEAD_DIM), jnp.bfloat16)
    own = pltpu.VMEM((HEADS, BLOCK, HEAD_DIM), jnp.bfloat16)
    attended, counts, losses = pl.pallas_call(
        kernel,
        name="exchange_and_attend",
        out_shape=(
            jax.ShapeDtypeStruct(queries.shape, jnp.bfloat16),
            jax.ShapeDtypeStruct((1, LANES), jnp.float32),
            jax.ShapeDtypeStruct((1, LANES), jnp.float32),
        ),
        in_specs=[anywhere] * 5 + [local],
        out_specs=(anywhere, local, local),
        scratch_shapes=[
            own,
            window,
            window,
            own,
            pltpu.VMEM((BLOCK, SPAN), jnp.float32),
            pltpu.VMEM(id_shape, jnp.int32),
            pltpu.VMEM(id_shape, jnp.int32),
            pltpu.VMEM((BLOCK, LANES), jnp.int32),
            pltpu.VMEM((BLOCK, LANES), jnp.int32),
            pltpu.VMEM((GROUP, 8, LANES), jnp.float32),
            pltpu.VMEM((NY, 8, LANES), jnp.float32),
            pltpu.VMEM((NZ, 8, LANES), jnp.float32),
            pltpu.SemaphoreType.DMA((2,)),
            pltpu.SemaphoreType.DMA((3,)),
            pltpu.SemaphoreType.DMA((3, HEADS)),
            pltpu.SemaphoreType.DMA((2,)),
            pltpu.SemaphoreType.DMA((2, HEADS)),
            pltpu.SemaphoreType.DMA,
            pltpu.SemaphoreType.DMA,
            pltpu.SemaphoreType.DMA((3,)),
            pltpu.SemaphoreType.DMA((3,)),
        ],
        compiler_params=pltpu.CompilerParams(
            collective_id=0, has_side_effects=True, vmem_limit_bytes=56 * 1024 * 1024
        ),
    )(queries, key_rows, values, doc_ids.reshape(id_shape), image_flags.reshape(id_shape), stats)
    return attended, counts.reshape(documents), losses.reshape(documents)


def solution(mesh):
    split = Mesh(mesh.devices.reshape(NZ, NY, NC, NX), AXES)
    return jax.shard_map(
        per_device,
        mesh=split,
        in_specs=(
            P(AXES, None),
            P(AXES, None),
            P(AXES, None),
            P(),
            P(),
            P(AXES),
            P(AXES),
        ),
        out_specs=(P(AXES, None), P(), P()),
        check_vma=False,
    )
```

time: 201 us -> 88.7 us (0.44)
  Pallas kernels: 0 us -> 81.2 us
  matrix products: 59.3 us -> 0 us
  blocking collectives: 48.7 us -> 0 us
  starting transfers between devices: 34.1 us -> 0 us
  waiting for transfers between devices: 25.2 us -> 0 us
  other arithmetic: 19.3 us -> 2.12 us
  local copies, waits for them, and re-layouts: 12.4 us -> 4.5 us
    pallas_call x0 -> x1, Pallas kernels: none -> 81.2 us  [per_device(): pl.pallas_call(kernel, name='exchange_and_attend', out_shape=(jax.ShapeDt...]
    dot_general x16 -> x0, matrix products: 59.3 us -> none  [the longest x8 37.1 us: attend(): lax.dot_general(query_head, key_head, (((1,), (1,)), ((), ())), preferred...]
    psum x4 -> x0, blocking collectives: 48.7 us -> none  [over_axes(): return functools.reduce(lax.psum, axes, value)]
    all_to_all x4 -> x0, waiting for transfers between devices: 25.2 us -> none  [the longest x1 17.5 us: per_device(): lax.all_to_all(key_rows, 'head', split_axis=1, concat_axis=0, tiled=True)]
    ppermute x4 -> x0, starting transfers between devices: 17.8 us -> none  [shifted(): return lax.ppermute(block, axis, route)]
    all_to_all x4 -> x0, starting transfers between devices: 16.3 us -> none  [the longest x1 4.84 us: per_device(): lax.all_to_all(key_rows, 'head', split_axis=1, concat_axis=0, tiled=True)]
    reduce_sum x9 -> x1, other arithmetic: 11.1 us -> 0.83 us  [per_device(): counts = jnp.sum(member.astype(jnp.float32), axis=0)]
    all_to_all x4 -> x0, local copies, waits for them, and re-layouts: 8.15 us -> none  [the longest x1 2.82 us: per_device(): lax.all_to_all(key_rows, 'head', split_axis=1, concat_axis=0, tiled=True)]
  transfers between devices with their start and end apart: 8 -> 0, of which waited for: 3 -> 0; matrix products, arithmetic and copies ran while one was open for 25% -> 0% of each run, Pallas kernels for 0% -> 0%
where the time goes in v1:
time: 88.7 us; the launch traced here: 88.5 us
  Pallas kernels  81.2 us (92%)
  local copies, waits for them, and re-layouts  4.5 us (5%)
  other arithmetic  2.12 us (2%)
    pallas_call x1, Pallas kernels, per_device(): pl.pallas_call(kernel, name='exchange_and_attend', out_shape=(jax.ShapeDt...  81.2 us
    unnamed x7, local copies, waits for them, and re-layouts  3.73 us

profile of v1, /device:TPU:1, one launch (start us, length us, event | category | flops | bytes accessed | tf_op | source)
XLA Modules:
  0.0 88.5 jit_solution(10335321040016808632)
XLA Ops:
  0.6 0.7 broadcast_compare_fusion
  1.3 0.8 dynamic_slice.3
  2.1 0.8 convert_reduce_fusion
  2.9 0.6 select_maximum_fusion.stat_ref
  3.5 81.2 %exchange_and_attend.1 = (bf16[192,4096]{1,0:T(8,128)(2,1)}, f32[1,128]{1,0:T(1,128)}, f32[1,128]{1,0:T(1,128)}) custom-call(bf16[192,4096]{1,0:T(8,128)(2,1)} %q_hbm.1, bf16[192,4096]{1,0:T(8,128)(2,1)} %k_hbm.1, bf16[192,4096]{1,0:T(8,128)(2,1)} %v_hbm.1, s32[384,128]{1,0:T(8,128)} %bitcast.6, s32[384,128]{1,0:T(8,128)} %bitcast.7, ...), custom_call_target="tpu_custom_call" | custom-call | tf_op jit(solution)/shard_map/exchange_and_attend/pallas_call | solution.py:313
  84.8 0.0 copy-start.1
  84.8 0.0 copy-start
  84.8 2.7 %copy.13 = bf16[192,4096]{1,0:T(8,128)(2,1)} copy(bf16[192,4096]{1,0:T(8,128)(2,1)} %get-tuple-element.14) | data formatting | bytes 3145728
  87.5 0.0 copy-done.1
  87.5 0.5 copy.14
  88.0 0.0 copy-done
  88.0 0.5 copy.15
Async XLA Ops:
  84.8 2.7 %copy-start.1 = (f32[1,128]{1,0:T(1,128)S(1)}, f32[1,128]{1,0:T(1,128)}, u32[]{:S(2)}) copy-start(f32[1,128]{1,0:T(1,128)} %get-tuple-element.7) | copy-start | bytes 1540
  84.8 3.2 %copy-start = (f32[1,128]{1,0:T(1,128)S(1)}, f32[1,128]{1,0:T(1,128)}, u32[]{:S(2)}) copy-start(f32[1,128]{1,0:T(1,128)} %get-tuple-element.8) | copy-start | bytes 1540

commit v2 on v1

--- a/solution.py
+++ b/solution.py
@@ -37,8 +37,9 @@
     v_hbm,
     docs_hbm,
     flags_hbm,
-    stat_ref,
-    out_hbm,
+    labels_hbm,
+    token_loss_hbm,
+    out_ref,
     count_ref,
     loss_ref,
     q_buf,
@@ -53,21 +54,30 @@
     slots_a,
     slots_b,
     slots_c,
+    labels,
+    token_loss,
     id_sem,
     in_send,
     in_recv,
-    halo_send,
-    halo_recv,
+    back_send,
+    back_recv,
+    ahead_send,
+    ahead_recv,
     out_send,
     out_recv,
     stat_send,
     stat_recv,
+    relay_send,
+    relay_recv,
 ):
     z, y, c, x = (lax.axis_index(name) for name in AXES)
     me = c * NX + x
     block = z * NY + y
+    has_after, has_before = block < BLOCKS - 1, block > 0
     after = lax.rem(block + 1, BLOCKS)
     before = lax.rem(block + BLOCKS - 1, BLOCKS)
+    has_upper, has_lower = z < NZ - 1, z > 0
+    upper, lower = lax.rem(z + 1, NZ), lax.rem(z + NZ - 1, NZ)
 
     def member(index):
         return {"z": z, "y": y, "c": lax.div(index, NX), "x": lax.rem(index, NX)}
@@ -84,18 +94,34 @@
     id_copies = [
         pltpu.make_async_copy(docs_hbm, docs, id_sem.at[0]),
         pltpu.make_async_copy(flags_hbm, flags, id_sem.at[1]),
+        pltpu.make_async_copy(labels_hbm, labels, id_sem.at[2]),
+        pltpu.make_async_copy(token_loss_hbm, token_loss, id_sem.at[3]),
     ]
     for copy in id_copies:
         copy.start()
 
     barrier = pltpu.get_barrier_semaphore()
     peers = [member(lax.rem(me + o, GROUP)) for o in range(1, GROUP)]
-    peers += [in_block(after), in_block(before)]
     peers += [along_y(lax.rem(y + o, NY)) for o in range(1, NY)]
-    peers += [along_z(lax.rem(z + o, NZ)) for o in range(1, NZ)]
     for peer in peers:
         pl.semaphore_signal(barrier, inc=1, device_id=peer, device_id_type=MESH)
-    pl.semaphore_wait(barrier, len(peers))
+    expected = len(peers)
+    for present, peer in (
+        (has_after, in_block(after)),
+        (has_before, in_block(before)),
+        (has_upper, along_z(upper)),
+        (has_lower, along_z(lower)),
+    ):
+        expected = expected + present.astype(jnp.int32)
+
+        @pl.when(present)
+        def _(peer=peer):
+            pl.semaphore_signal(barrier, inc=1, device_id=peer, device_id_type=MESH)
+
+    pl.semaphore_wait(barrier, expected)
+
+    def drain(ref, sem):
+        pltpu.make_async_copy(ref, ref, sem).wait()
 
     sources = (k_hbm, v_hbm, q_hbm)
     targets = (k_buf, v_buf, q_buf)
@@ -131,20 +157,40 @@
         rows = targets[array].at[head, pl.ds(bases[array], BLOCK), :]
         pltpu.make_async_copy(rows, rows, in_recv.at[array, head]).wait()
 
+    def halos(array, head):
+        return (
+            (has_after, has_before, BACK, FRONT + BLOCK - BACK, FRONT - BACK, after, back_send, back_recv),
+            (has_before, has_after, AHEAD, FRONT, FRONT + BLOCK, before, ahead_send, ahead_recv),
+        )
+
     def start_halo(array, head):
         buffer = targets[array]
-        for rows, first, target, peer in (
-            (BACK, FRONT + BLOCK - BACK, FRONT - BACK, after),
-            (AHEAD, FRONT, FRONT + BLOCK, before),
-        ):
-            pltpu.make_async_remote_copy(
-                src_ref=buffer.at[head, pl.ds(first, rows), :],
-                dst_ref=buffer.at[head, pl.ds(target, rows), :],
-                send_sem=halo_send.at[array],
-                recv_sem=halo_recv.at[array, head],
-                device_id=in_block(peer),
-                device_id_type=MESH,
-            ).start()
+        for sends, _, rows, first, target, peer, send_sem, recv_sem in halos(array, head):
+
+            @pl.when(sends)
+            def _():
+                pltpu.make_async_remote_copy(
+                    src_ref=buffer.at[head, pl.ds(first, rows), :],
+                    dst_ref=buffer.at[head, pl.ds(target, rows), :],
+                    send_sem=send_sem.at[array],
+                    recv_sem=recv_sem.at[array, head],
+                    device_id=in_block(peer),
+                    device_id_type=MESH,
+                ).start()
+
+    def wait_halo(array, head):
+        for _, receives, rows, _, target, _, _, recv_sem in halos(array, head):
+
+            @pl.when(receives)
+            def _():
+                drain(targets[array].at[head, pl.ds(target, rows), :], recv_sem.at[array, head])
+
+    def drain_halo(array):
+        for sends, _, rows, _, _, _, send_sem, _ in halos(array, 0):
+
+            @pl.when(sends)
+            def _():
+                drain(targets[array].at[:, pl.ds(0, rows), :], send_sem.at[array])
 
     def stage_send(number, slots, own, size, peer_of):
         def send(o, carry):
@@ -168,24 +214,84 @@
             total = total + slots[i]
         return total
 
-    def after_groups(group):
-        if group == 0:
+    def relays(step):
+        return (
+            (has_upper & (z >= step), z - step, has_lower & (z >= step + 1), z - 1 - step, upper, 0),
+            (has_lower & (z + step < NZ), z + step, has_upper & (z + step + 1 < NZ), z + 1 + step, lower, 1),
+        )
+
+    def relay_copy(step, slot, peer, way):
+        return pltpu.make_async_remote_copy(
+            src_ref=slots_c.at[slot],
+            dst_ref=slots_c.at[slot],
+            send_sem=relay_send.at[way, step],
+            recv_sem=relay_recv.at[way, step],
+            device_id=along_z(peer),
+            device_id_type=MESH,
+        )
+
+    def relay_start(step):
+        for sends, slot, _, _, peer, way in relays(step):
+
+            @pl.when(sends)
+            def _():
+                relay_copy(step, slot, peer, way).start()
+
+    def relay_wait(step):
+        for _, _, receives, slot, peer, way in relays(step):
+
+            @pl.when(receives)
+            def _():
+                drain(slots_c.at[slot], relay_recv.at[way, step])
+
+    def relay_drain(step):
+        for sends, slot, _, _, peer, way in relays(step):
+
+            @pl.when(sends)
+            def _():
+                drain(slots_c.at[slot], relay_send.at[way, step])
+
+    def document_partials():
+        first = lax.div(block * BLOCK + me * STRIP, LANES)
+        pair = jnp.concatenate([docs[pl.ds(first, 1), :], docs[pl.ds(first + 1, 1), :]], axis=1)
+        half = jnp.concatenate([pair[:, 64:], pair[:, :64]], axis=1)
+        doc = jnp.where(lax.rem(me, 2) == 1, half, pair)[:, :STRIP]
+        weight = jnp.where(labels[...] >= 0, 1.0, 0.0)
+        lines = lax.broadcasted_iota(jnp.int32, (8, STRIP), 0)
+        terms = jnp.where(lines == 0, weight, jnp.where(lines == 1, weight * token_loss[...], 0.0))
+        hit = jnp.where(lax.broadcasted_iota(jnp.int32, (LANES, STRIP), 0) == doc, 1.0, 0.0)
+        return lax.dot_general(
+            terms,
+            hit,
+            (((1,), (1,)), ((), ())),
+            precision=lax.Precision.HIGHEST,
+            preferred_element_type=jnp.float32,
+        )
+
+    def totals_step(point):
+        if point == 0:
             for copy in id_copies:
                 copy.wait()
+            slots_a[me] = document_partials()
+            stage_send(0, slots_a, me, GROUP, member)
             make_query_ids()
-        elif group == 1:
-            total = stage_sum(0, slots_a, GROUP)
-            slots_b[y] = total
+        elif point == 1:
+            slots_b[y] = stage_sum(0, slots_a, GROUP)
             stage_send(1, slots_b, y, NY, along_y)
-        elif group == 3:
-            total = stage_sum(1, slots_b, NY)
-            slots_c[z] = total
-            stage_send(2, slots_c, z, NZ, along_z)
-        elif group == 5:
-            total = stage_sum(2, slots_c, NZ)
-            counts = total[0:1]
-            count_ref[...] = counts
-            loss_ref[...] = total[1:2] / jnp.maximum(counts, 1.0)
+        elif point == 2:
+            slots_c[z] = stage_sum(1, slots_b, NY)
+            relay_start(0)
+        else:
+            relay_wait(point - 3)
+            if point - 2 < NZ - 1:
+                relay_start(point - 2)
+            else:
+                total = slots_c[0]
+                for i in range(1, NZ):
+                    total = total + slots_c[i]
+                counts = total[0:1]
+                count_ref[...] = counts
+                loss_ref[...] = total[1:2] / jnp.maximum(counts, 1.0)
 
     def id_row(row):
         at = pl.ds(lax.rem(block * (BLOCK // LANES) + row + BLOCKS * (BLOCK // LANES), BLOCKS * (BLOCK // LANES)), 1)
@@ -234,7 +340,7 @@
         )
         o_buf[head, rows, :] = (mixed / total).astype(jnp.bfloat16)
         columns = pl.ds(pl.multiple_of(me * HEADS * HEAD_DIM + head * HEAD_DIM, LANES), HEAD_DIM)
-        source, target = o_buf.at[head, rows, :], out_hbm.at[:, columns]
+        source, target = o_buf.at[head, rows, :], out_ref.at[:, columns]
 
         @pl.when(strip == me)
         def _():
@@ -253,25 +359,32 @@
 
     for group in range(DEPTH):
         start_group(group)
-    slots_a[me] = stat_ref[...]
-    stage_send(0, slots_a, me, GROUP, member)
 
     edge = jnp.zeros((HEADS, 64, HEAD_DIM), jnp.bfloat16)
     for buffer in (k_buf, v_buf):
         buffer[:, 0 : FRONT - BACK, :] = edge
         buffer[:, FRONT + BLOCK + AHEAD : WINDOW, :] = edge
 
+    @pl.when(block == 0)
+    def _():
+        for buffer in (k_buf, v_buf):
+            buffer[:, FRONT - BACK : FRONT, :] = jnp.zeros((HEADS, BACK, HEAD_DIM), jnp.bfloat16)
+
+    @pl.when(block == BLOCKS - 1)
+    def _():
+        for buffer in (k_buf, v_buf):
+            buffer[:, FRONT + BLOCK : FRONT + BLOCK + AHEAD, :] = jnp.zeros((HEADS, AHEAD, HEAD_DIM), jnp.bfloat16)
+
     for group in range(2 * HEADS):
         wait_group(group)
         start_halo(*divmod(group, HEADS))
         start_group(group + DEPTH)
-        after_groups(group)
+        totals_step(group)
         make_bias(group)
 
     for head in range(HEADS):
         for array in range(2):
-            rows = targets[array].at[head, pl.ds(0, BACK + AHEAD), :]
-            pltpu.make_async_copy(rows, rows, halo_recv.at[array, head]).wait()
+            wait_halo(array, head)
         group = 2 * HEADS + head
         wait_group(group)
         if group + DEPTH < 3 * HEADS:
@@ -282,29 +395,23 @@
             return carry
 
         lax.fori_loop(1, GROUP + 1, step, 0)
-
-    def drain(ref, sem):
-        pltpu.make_async_copy(ref, ref, sem).wait()
+        if head < 2:
+            totals_step(2 * HEADS + head)
 
     for array in range(3):
         drain(targets[array].at[:, pl.ds(0, BLOCK - STRIP), :], in_send.at[array])
     for array in range(2):
-        drain(targets[array].at[:, pl.ds(0, BACK + AHEAD), :], halo_send.at[array])
-    for number, slots, size in ((0, slots_a, GROUP), (1, slots_b, NY), (2, slots_c, NZ)):
+        drain_halo(array)
+    for number, slots, size in ((0, slots_a, GROUP), (1, slots_b, NY)):
         drain(slots.at[pl.ds(0, size - 1)], stat_send.at[number])
+    for number in range(NZ - 1):
+        relay_drain(number)
     drain(o_buf.at[:, pl.ds(0, BLOCK - STRIP), :], out_send)
-    drain(out_hbm, out_recv)
+    drain(out_ref, out_recv)
 
 
 def per_device(queries, key_rows, values, doc_ids, image_flags, labels, token_loss):
-    rows = labels.shape[0]
-    place = ((lax.axis_index("z") * NY + lax.axis_index("y")) * NC + lax.axis_index("c")) * NX + lax.axis_index("x")
-    local_docs = lax.dynamic_slice_in_dim(doc_ids, place * rows, rows)
     documents = doc_ids.shape[0] // DOC_MEAN
-    member = (local_docs[:, None] == jnp.arange(documents, dtype=jnp.int32)[None, :]) & (labels[:, None] >= 0)
-    counts = jnp.sum(member.astype(jnp.float32), axis=0)
-    sums = jnp.sum(jnp.where(member, token_loss[:, None], jnp.float32(0.0)), axis=0)
-    stats = jnp.pad(jnp.stack([counts, sums]), ((0, 6), (0, 0)))
     id_shape = (BLOCKS * BLOCK // LANES, LANES)
     anywhere = pl.BlockSpec(memory_space=pl.ANY)
     local = pl.BlockSpec(memory_space=pltpu.VMEM)
@@ -314,12 +421,12 @@
         kernel,
         name="exchange_and_attend",
         out_shape=(
-            jax.ShapeDtypeStruct(queries.shape, jnp.bfloat16),
-            jax.ShapeDtypeStruct((1, LANES), jnp.float32),
-            jax.ShapeDtypeStruct((1, LANES), jnp.float32),
+            pltpu.VMEM(queries.shape, jnp.bfloat16),
+            pltpu.VMEM((1, LANES), jnp.float32),
+            pltpu.VMEM((1, LANES), jnp.float32),
         ),
-        in_specs=[anywhere] * 5 + [local],
-        out_specs=(anywhere, local, local),
+        in_specs=[anywhere] * 7,
+        out_specs=(local, local, local),
         scratch_shapes=[
             own,
             window,
@@ -333,20 +440,39 @@
             pltpu.VMEM((GROUP, 8, LANES), jnp.float32),
             pltpu.VMEM((NY, 8, LANES), jnp.float32),
             pltpu.VMEM((NZ, 8, LANES), jnp.float32),
-            pltpu.SemaphoreType.DMA((2,)),
+            pltpu.VMEM((1, STRIP), jnp.int32),
+            pltpu.VMEM((1, STRIP), jnp.float32),
+            pltpu.SemaphoreType.DMA((4,)),
             pltpu.SemaphoreType.DMA((3,)),
             pltpu.SemaphoreType.DMA((3, HEADS)),
             pltpu.SemaphoreType.DMA((2,)),
             pltpu.SemaphoreType.DMA((2, HEADS)),
+            pltpu.SemaphoreType.DMA((2,)),
+            pltpu.SemaphoreType.DMA((2, HEADS)),
             pltpu.SemaphoreType.DMA,
             pltpu.SemaphoreType.DMA,
-            pltpu.SemaphoreType.DMA((3,)),
-            pltpu.SemaphoreType.DMA((3,)),
+            pltpu.SemaphoreType.DMA((2,)),
+            pltpu.SemaphoreType.DMA((2,)),
+            pltpu.SemaphoreType.DMA((2, NZ - 1)),
+            pltpu.SemaphoreType.DMA((2, NZ - 1)),
         ],
         compiler_params=pltpu.CompilerParams(
-            collective_id=0, has_side_effects=True, vmem_limit_bytes=56 * 1024 * 1024
+            collective_id=0, has_side_effects=True, vmem_limit_bytes=40 * 1024 * 1024
         ),
-    )(queries, key_rows, values, doc_ids.reshape(id_shape), image_flags.reshape(id_shape), stats)
+    )(
+        *(
+            pltpu.with_memory_space_constraint(array, pltpu.HBM)
+            for array in (
+                queries,
+                key_rows,
+                values,
+                doc_ids.reshape(id_shape),
+                image_flags.reshape(id_shape),
+                labels.reshape(1, STRIP),
+                token_loss.reshape(1, STRIP),
+            )
+        )
+    )
     return attended, counts.reshape(documents), losses.reshape(documents)
 
 

time: 88.7 us -> 78.7 us (0.89)
  Pallas kernels: 81.2 us -> 75.4 us
  local copies, waits for them, and re-layouts: 4.5 us -> 2.17 us
  other arithmetic: 2.12 us -> 0 us
    pallas_call x1, Pallas kernels: 81.2 us -> 75.4 us  [per_device(): pl.pallas_call(kernel, name='exchange_and_attend', out_shape=(pltpu.VMEM(...]
    unnamed x7 -> x3, local copies, waits for them, and re-layouts: 3.73 us -> 2.17 us
where the time goes in v2:
time: 78.7 us; the launch traced here: 78.2 us
  Pallas kernels  75.4 us (96%)
  local copies, waits for them, and re-layouts  2.17 us (3%)
    pallas_call x1, Pallas kernels, per_device(): pl.pallas_call(kernel, name='exchange_and_attend', out_shape=(pltpu.VMEM(...  75.4 us
    unnamed x3, local copies, waits for them, and re-layouts  2.17 us

profile of v2, /device:TPU:1, one launch (start us, length us, event | category | flops | bytes accessed | tf_op | source)
XLA Modules:
  0.0 78.2 jit_solution(10857185975487760499)
XLA Ops:
  0.6 75.4 %exchange_and_attend.1 = (bf16[192,4096]{1,0:T(8,128)(2,1)S(1)}, f32[1,128]{1,0:T(1,128)S(1)}, f32[1,128]{1,0:T(1,128)S(1)}) custom-call(bf16[192,4096]{1,0:T(8,128)(2,1)} %q_hbm.1, bf16[192,4096]{1,0:T(8,128)(2,1)} %k_hbm.1, bf16[192,4096]{1,0:T(8,128)(2,1)} %v_hbm.1, s32[384,128]{1,0:T(8,128)} %bitcast.8, s32[384,128]{1,0:T(8,128)} %bitcast.9, ...), custom_call_target="tpu_custom_call" | custom-call | tf_op jit(solution)/shard_map/exchange_and_attend/pallas_call | solution.py:420
  76.1 1.1 %copy.13 = bf16[192,4096]{1,0:T(8,128)(2,1)} copy(bf16[192,4096]{1,0:T(8,128)(2,1)S(1)} %get-tuple-element.9) | data formatting | bytes 3145728
  77.2 0.5 copy.14
  77.7 0.5 copy.15

commit v3 on v2

--- a/solution.py
+++ b/solution.py
@@ -408,6 +408,31 @@
         relay_drain(number)
     drain(o_buf.at[:, pl.ds(0, BLOCK - STRIP), :], out_send)
     drain(out_ref, out_recv)
+
+
+def store_kernel(chunks, attended, counts, losses, attended_out, counts_out, losses_out, sems):
+    rows = attended.shape[0] // chunks
+    parts = [(attended.at[pl.ds(i * rows, rows)], attended_out.at[pl.ds(i * rows, rows)]) for i in range(chunks)]
+    parts += [(counts, counts_out), (losses, losses_out)]
+    copies = [pltpu.make_async_copy(source, target, sems.at[i]) for i, (source, target) in enumerate(parts)]
+    for copy in copies:
+        copy.start()
+    for copy in copies:
+        copy.wait()
+
+
+def store(attended, counts, losses, chunks=4):
+    local = pl.BlockSpec(memory_space=pltpu.VMEM)
+    anywhere = pl.BlockSpec(memory_space=pl.ANY)
+    results = (attended, counts, losses)
+    return pl.pallas_call(
+        functools.partial(store_kernel, chunks),
+        name="store_results",
+        out_shape=tuple(jax.ShapeDtypeStruct(a.shape, a.dtype) for a in results),
+        in_specs=[local] * 3,
+        out_specs=(anywhere,) * 3,
+        scratch_shapes=[pltpu.SemaphoreType.DMA((chunks + 2,))],
+    )(*(pltpu.with_memory_space_constraint(a, pltpu.VMEM) for a in results))
 
 
 def per_device(queries, key_rows, values, doc_ids, image_flags, labels, token_loss):
@@ -473,6 +498,7 @@
             )
         )
     )
+    attended, counts, losses = store(attended, counts, losses)
     return attended, counts.reshape(documents), losses.reshape(documents)
 
 

time: 78.7 us -> 77.7 us (0.987)
  local copies, waits for them, and re-layouts: 2.17 us -> 0 us
  Pallas kernels: 75.4 us -> 76.6 us
    unnamed x3 -> x0, local copies, waits for them, and re-layouts: 2.17 us -> none
    pallas_call x0 -> x1, Pallas kernels: none -> 1.19 us  [store(): pl.pallas_call(functools.partial(store_kernel, chunks), name='store_resul...]
where the time goes in v3:
time: 77.7 us; the launch traced here: 77.3 us
  Pallas kernels  76.6 us (99%)
    pallas_call x1, Pallas kernels, per_device(): pl.pallas_call(kernel, name='exchange_and_attend', out_shape=(pltpu.VMEM(...  75.4 us

profile of v3, /device:TPU:1, one launch (start us, length us, event | category | flops | bytes accessed | tf_op | source)
XLA Modules:
  0.0 77.3 jit_solution(8406699988377322508)
XLA Ops:
  0.6 75.4 %exchange_and_attend.1 = (bf16[192,4096]{1,0:T(8,128)(2,1)S(1)}, f32[1,128]{1,0:T(1,128)S(1)}, f32[1,128]{1,0:T(1,128)S(1)}) custom-call(bf16[192,4096]{1,0:T(8,128)(2,1)} %q_hbm.1, bf16[192,4096]{1,0:T(8,128)(2,1)} %k_hbm.1, bf16[192,4096]{1,0:T(8,128)(2,1)} %v_hbm.1, s32[384,128]{1,0:T(8,128)} %bitcast.6, s32[384,128]{1,0:T(8,128)} %bitcast.7, ...), custom_call_target="tpu_custom_call" | custom-call | tf_op jit(solution)/shard_map/exchange_and_attend/pallas_call | solution.py:445
  76.1 1.2 %store_results.1 = (bf16[192,4096]{1,0:T(8,128)(2,1)}, f32[1,128]{1,0:T(1,128)}, f32[1,128]{1,0:T(1,128)}) custom-call(bf16[192,4096]{1,0:T(8,128)(2,1)S(1)} %get-tuple-element.9.attended, f32[1,128]{1,0:T(1,128)S(1)} %get-tuple-element.10.counts, f32[1,128]{1,0:T(1,128)S(1)} %get-tuple-element.11.losses), custom_call_target="tpu_custom_call" | custom-call | tf_op jit(solution)/shard_map/store_results/pallas_call | solution.py:428

commit v4 on v3

--- a/solution.py
+++ b/solution.py
@@ -69,6 +69,8 @@
     stat_recv,
     relay_send,
     relay_recv,
+    met_far,
+    met_upper,
 ):
     z, y, c, x = (lax.axis_index(name) for name in AXES)
     me = c * NX + x
@@ -101,24 +103,32 @@
         copy.start()
 
     barrier = pltpu.get_barrier_semaphore()
-    peers = [member(lax.rem(me + o, GROUP)) for o in range(1, GROUP)]
-    peers += [along_y(lax.rem(y + o, NY)) for o in range(1, NY)]
-    for peer in peers:
-        pl.semaphore_signal(barrier, inc=1, device_id=peer, device_id_type=MESH)
-    expected = len(peers)
-    for present, peer in (
-        (has_after, in_block(after)),
-        (has_before, in_block(before)),
-        (has_upper, along_z(upper)),
-        (has_lower, along_z(lower)),
-    ):
-        expected = expected + present.astype(jnp.int32)
-
-        @pl.when(present)
-        def _(peer=peer):
-            pl.semaphore_signal(barrier, inc=1, device_id=peer, device_id_type=MESH)
-
-    pl.semaphore_wait(barrier, expected)
+    def toward(steps, other):
+        return lax.rem(c + other, NC) * NX + lax.rem(x + steps, NX)
+
+    def tell(sem, present, peer):
+        def signal():
+            pl.semaphore_signal(sem, inc=1, device_id=peer, device_id_type=MESH)
+
+        if present is None:
+            signal()
+        else:
+            pl.when(present)(signal)
+
+    for steps, other in ((1, 0), (NX - 1, 0), (1, 1), (NX - 1, 1), (0, 1)):
+        tell(barrier, None, member(toward(steps, other)))
+    for o in range(NY):
+        tell(barrier, y < o, along_y(o))
+    tell(barrier, has_upper, along_z(upper))
+    tell(barrier, has_upper & (y == NY - 1), in_block(after))
+    from_lower = jnp.where(has_lower, jnp.where(y == 0, 2, 1), 0) + y
+    from_upper = jnp.where(has_upper, jnp.where(y == NY - 1, 2, 1), 0) + NY - 1 - y
+    pl.semaphore_wait(barrier, 5 + from_lower)
+    tell(met_far, None, member(toward(1, 0)))
+    for o in range(NY):
+        tell(met_upper, y > o, along_y(o))
+    tell(met_upper, has_lower, along_z(lower))
+    tell(met_upper, has_lower & (y == 0), in_block(before))
 
     def drain(ref, sem):
         pltpu.make_async_copy(ref, ref, sem).wait()
@@ -135,8 +145,7 @@
     def start_group(group):
         array, head = divmod(group, HEADS)
 
-        def send(o, carry):
-            owner = lax.rem(me + o, GROUP)
+        def send(owner):
             source, target = piece(array, head, owner)
             pltpu.make_async_remote_copy(
                 src_ref=source,
@@ -146,9 +155,20 @@
                 device_id=member(owner),
                 device_id_type=MESH,
             ).start()
+
+        def near(o, carry):
+            send(toward(1 + (NX - 2) * lax.rem(o, 2), lax.div(o, 2)))
             return carry
 
-        lax.fori_loop(1, GROUP, send, 0)
+        def far(o, carry):
+            send(toward(2, o))
+            return carry
+
+        lax.fori_loop(0, 2 * NC, near, 0)
+        if group == 0:
+            pl.semaphore_wait(met_far, 1)
+        lax.fori_loop(0, NC, far, 0)
+        send(toward(0, 1))
         source, target = piece(array, head, me)
         pltpu.make_async_copy(source, target, in_recv.at[array, head]).start()
 
@@ -377,6 +397,12 @@
 
     for group in range(2 * HEADS):
         wait_group(group)
+        if group == 0:
+
+            @pl.when(from_upper > 0)
+            def _():
+                pl.semaphore_wait(met_upper, from_upper)
+
         start_halo(*divmod(group, HEADS))
         start_group(group + DEPTH)
         totals_step(group)
@@ -480,6 +506,8 @@
             pltpu.SemaphoreType.DMA((2,)),
             pltpu.SemaphoreType.DMA((2, NZ - 1)),
             pltpu.SemaphoreType.DMA((2, NZ - 1)),
+            pltpu.SemaphoreType.REGULAR,
+            pltpu.SemaphoreType.REGULAR,
         ],
         compiler_params=pltpu.CompilerParams(
             collective_id=0, has_side_effects=True, vmem_limit_bytes=40 * 1024 * 1024

time: 77.7 us -> 77.7 us (level); the launches traced: 77.3 us -> 76.4 us
  Pallas kernels: 76.6 us -> 75.8 us
    pallas_call x1, Pallas kernels: 75.4 us -> 74.6 us  [per_device(): pl.pallas_call(kernel, name='exchange_and_attend', out_shape=(pltpu.VMEM(...]
where the time goes in v4:
time: 77.7 us; the launch traced here: 76.4 us
  Pallas kernels  75.8 us (98%)
    pallas_call x1, Pallas kernels, per_device(): pl.pallas_call(kernel, name='exchange_and_attend', out_shape=(pltpu.VMEM(...  74.6 us

profile of v4, /device:TPU:1, one launch (start us, length us, event | category | flops | bytes accessed | tf_op | source)
XLA Modules:
  0.0 76.4 jit_solution(1934947915127417650)
XLA Ops:
  0.6 74.6 %exchange_and_attend.1 = (bf16[192,4096]{1,0:T(8,128)(2,1)S(1)}, f32[1,128]{1,0:T(1,128)S(1)}, f32[1,128]{1,0:T(1,128)S(1)}) custom-call(bf16[192,4096]{1,0:T(8,128)(2,1)} %q_hbm.1, bf16[192,4096]{1,0:T(8,128)(2,1)} %k_hbm.1, bf16[192,4096]{1,0:T(8,128)(2,1)} %v_hbm.1, s32[384,128]{1,0:T(8,128)} %bitcast.6, s32[384,128]{1,0:T(8,128)} %bitcast.7, ...), custom_call_target="tpu_custom_call" | custom-call | tf_op jit(solution)/shard_map/exchange_and_attend/pallas_call | solution.py:471
  75.2 1.2 %store_results.1 = (bf16[192,4096]{1,0:T(8,128)(2,1)}, f32[1,128]{1,0:T(1,128)}, f32[1,128]{1,0:T(1,128)}) custom-call(bf16[192,4096]{1,0:T(8,128)(2,1)S(1)} %get-tuple-element.9.attended, f32[1,128]{1,0:T(1,128)S(1)} %get-tuple-element.10.counts, f32[1,128]{1,0:T(1,128)S(1)} %get-tuple-element.11.losses), custom_call_target="tpu_custom_call" | custom-call | tf_op jit(solution)/shard_map/store_results/pallas_call | solution.py:454

commit v5 on v4

--- a/solution.py
+++ b/solution.py
@@ -21,7 +21,6 @@
 FRONT = 768
 SPAN = 1536
 WINDOW = FRONT + BLOCK + 640
-DEPTH = 3
 LANES = 128
 AXES = ("z", "y", "c", "x")
 MESH = pl.DeviceIdType.MESH
@@ -56,6 +55,8 @@
     slots_c,
     labels,
     token_loss,
+    stage,
+    stage_sem,
     id_sem,
     in_send,
     in_recv,
@@ -99,7 +100,11 @@
         pltpu.make_async_copy(labels_hbm, labels, id_sem.at[2]),
         pltpu.make_async_copy(token_loss_hbm, token_loss, id_sem.at[3]),
     ]
-    for copy in id_copies:
+    stage_copies = [
+        pltpu.make_async_copy(source, stage.at[array], stage_sem.at[array])
+        for array, source in enumerate((k_hbm, v_hbm, q_hbm))
+    ]
+    for copy in stage_copies:
         copy.start()
 
     barrier = pltpu.get_barrier_semaphore()
@@ -115,36 +120,39 @@
         else:
             pl.when(present)(signal)
 
-    for steps, other in ((1, 0), (NX - 1, 0), (1, 1), (NX - 1, 1), (0, 1)):
-        tell(barrier, None, member(toward(steps, other)))
-    for o in range(NY):
-        tell(barrier, y < o, along_y(o))
+    def meet_near(o, carry):
+        tell(barrier, None, member(toward(jnp.where(o == 4, 0, 1 + (NX - 2) * lax.rem(o, 2)), jnp.where(o < 2, 0, 1))))
+        return carry
+
+    def meet_higher(o, carry):
+        tell(barrier, None, along_y(o))
+        return carry
+
+    def answer_lower(o, carry):
+        tell(met_upper, None, along_y(o))
+        return carry
+
+    lax.fori_loop(0, 5, meet_near, 0)
+    lax.fori_loop(y + 1, NY, meet_higher, 0)
     tell(barrier, has_upper, along_z(upper))
     tell(barrier, has_upper & (y == NY - 1), in_block(after))
     from_lower = jnp.where(has_lower, jnp.where(y == 0, 2, 1), 0) + y
     from_upper = jnp.where(has_upper, jnp.where(y == NY - 1, 2, 1), 0) + NY - 1 - y
     pl.semaphore_wait(barrier, 5 + from_lower)
     tell(met_far, None, member(toward(1, 0)))
-    for o in range(NY):
-        tell(met_upper, y > o, along_y(o))
-    tell(met_upper, has_lower, along_z(lower))
-    tell(met_upper, has_lower & (y == 0), in_block(before))
 
     def drain(ref, sem):
         pltpu.make_async_copy(ref, ref, sem).wait()
 
-    sources = (k_hbm, v_hbm, q_hbm)
     targets = (k_buf, v_buf, q_buf)
     bases = (FRONT, FRONT, 0)
 
     def piece(array, head, owner):
         columns = pl.ds(pl.multiple_of(owner * HEADS * HEAD_DIM + head * HEAD_DIM, LANES), HEAD_DIM)
         rows = pl.ds(pl.multiple_of(bases[array] + me * STRIP, 64), STRIP)
-        return sources[array].at[:, columns], targets[array].at[head, rows, :]
-
-    def start_group(group):
-        array, head = divmod(group, HEADS)
-
+        return stage.at[array, :, columns], targets[array].at[head, rows, :]
+
+    def start_group(array, head, first=None):
         def send(owner):
             source, target = piece(array, head, owner)
             pltpu.make_async_remote_copy(
@@ -165,15 +173,18 @@
             return carry
 
         lax.fori_loop(0, 2 * NC, near, 0)
-        if group == 0:
-            pl.semaphore_wait(met_far, 1)
+        if first is not None:
+
+            @pl.when(first)
+            def _():
+                pl.semaphore_wait(met_far, 1)
+
         lax.fori_loop(0, NC, far, 0)
         send(toward(0, 1))
         source, target = piece(array, head, me)
         pltpu.make_async_copy(source, target, in_recv.at[array, head]).start()
 
-    def wait_group(group):
-        array, head = divmod(group, HEADS)
+    def wait_group(array, head):
         rows = targets[array].at[head, pl.ds(bases[array], BLOCK), :]
         pltpu.make_async_copy(rows, rows, in_recv.at[array, head]).wait()
 
@@ -288,30 +299,37 @@
             preferred_element_type=jnp.float32,
         )
 
-    def totals_step(point):
-        if point == 0:
+    def totals_start(head):
+        @pl.when(head == 0)
+        def _():
             for copy in id_copies:
                 copy.wait()
             slots_a[me] = document_partials()
             stage_send(0, slots_a, me, GROUP, member)
             make_query_ids()
-        elif point == 1:
+
+        @pl.when(head == 1)
+        def _():
             slots_b[y] = stage_sum(0, slots_a, GROUP)
             stage_send(1, slots_b, y, NY, along_y)
-        elif point == 2:
+
+        @pl.when(head == 2)
+        def _():
             slots_c[z] = stage_sum(1, slots_b, NY)
             relay_start(0)
-        else:
-            relay_wait(point - 3)
-            if point - 2 < NZ - 1:
-                relay_start(point - 2)
-            else:
-                total = slots_c[0]
-                for i in range(1, NZ):
-                    total = total + slots_c[i]
-                counts = total[0:1]
-                count_ref[...] = counts
-                loss_ref[...] = total[1:2] / jnp.maximum(counts, 1.0)
+
+        @pl.when(head == 3)
+        def _():
+            relay_wait(0)
+            relay_start(1)
+
+    def totals_end():
+        total = slots_c[0]
+        for i in range(1, NZ):
+            total = total + slots_c[i]
+        counts = total[0:1]
+        count_ref[...] = counts
+        loss_ref[...] = total[1:2] / jnp.maximum(counts, 1.0)
 
     def id_row(row):
         at = pl.ds(lax.rem(block * (BLOCK // LANES) + row + BLOCKS * (BLOCK // LANES), BLOCKS * (BLOCK // LANES)), 1)
@@ -377,61 +395,115 @@
                 device_id_type=MESH,
             ).start()
 
-    for group in range(DEPTH):
-        start_group(group)
-
-    edge = jnp.zeros((HEADS, 64, HEAD_DIM), jnp.bfloat16)
-    for buffer in (k_buf, v_buf):
-        buffer[:, 0 : FRONT - BACK, :] = edge
-        buffer[:, FRONT + BLOCK + AHEAD : WINDOW, :] = edge
-
-    @pl.when(block == 0)
-    def _():
-        for buffer in (k_buf, v_buf):
-            buffer[:, FRONT - BACK : FRONT, :] = jnp.zeros((HEADS, BACK, HEAD_DIM), jnp.bfloat16)
-
-    @pl.when(block == BLOCKS - 1)
-    def _():
-        for buffer in (k_buf, v_buf):
-            buffer[:, FRONT + BLOCK : FRONT + BLOCK + AHEAD, :] = jnp.zeros((HEADS, AHEAD, HEAD_DIM), jnp.bfloat16)
-
-    for group in range(2 * HEADS):
-        wait_group(group)
-        if group == 0:
-
-            @pl.when(from_upper > 0)
-            def _():
-                pl.semaphore_wait(met_upper, from_upper)
-
-        start_halo(*divmod(group, HEADS))
-        start_group(group + DEPTH)
-        totals_step(group)
-        make_bias(group)
-
-    for head in range(HEADS):
+    def first_groups(head, carry):
+        start_group(0, head, first=head == 0)
+        return carry
+
+    stage_copies[0].wait()
+    lax.fori_loop(0, HEADS - 1, first_groups, 0)
+    lax.fori_loop(0, y, answer_lower, 0)
+    tell(met_upper, has_lower, along_z(lower))
+    tell(met_upper, has_lower & (y == 0), in_block(before))
+    for copy in id_copies:
+        copy.start()
+
+    def clear(head, carry):
+        def rows(first, count):
+            for buffer in (k_buf, v_buf):
+                buffer[head, first : first + count, :] = jnp.zeros((count, HEAD_DIM), jnp.bfloat16)
+
+        rows(0, FRONT - BACK)
+        rows(FRONT + BLOCK + AHEAD, WINDOW - FRONT - BLOCK - AHEAD)
+
+        @pl.when(block == 0)
+        def _():
+            rows(FRONT - BACK, BACK)
+
+        @pl.when(block == BLOCKS - 1)
+        def _():
+            rows(FRONT + BLOCK, AHEAD)
+
+        return carry
+
+    lax.fori_loop(0, HEADS, clear, 0)
+
+    for array in range(2):
+
+        def spread(head, carry, array=array):
+            wait_group(array, head)
+            if array == 0:
+
+                @pl.when((head == 0) & (from_upper > 0))
+                def _():
+                    pl.semaphore_wait(met_upper, from_upper)
+
+            start_halo(array, head)
+
+            @pl.when(head == 0)
+            def _():
+                start_group(array, HEADS - 1)
+                stage_copies[array + 1].wait()
+
+            @pl.when(head > 0)
+            def _():
+                start_group(array + 1, head - 1)
+
+            if array == 0:
+                totals_start(head)
+            else:
+                relay_wait(head + 1)
+                relay_start(head + 2)
+            make_bias(array * HEADS + head)
+            return carry
+
+        lax.fori_loop(0, HEADS, spread, 0)
+
+    def one_head(head, carry):
         for array in range(2):
             wait_halo(array, head)
-        group = 2 * HEADS + head
-        wait_group(group)
-        if group + DEPTH < 3 * HEADS:
-            start_group(group + DEPTH)
-
-        def step(i, carry, head=head):
-            attend(head, lax.rem(me + i, GROUP))
+        wait_group(2, head)
+
+        @pl.when(head == 0)
+        def _():
+            start_group(2, HEADS - 1)
+
+        def step(i, carry):
+            j = i - 1
+            steps = jnp.where(j < 2, 2, jnp.where(j < 6, 1 + (NX - 2) * lax.rem(j, 2), 0))
+            other = jnp.where(j < 2, j, jnp.where(j < 6, lax.div(j - 2, 2), 1 - lax.rem(j, 2)))
+            attend(head, toward(steps, other))
             return carry
 
         lax.fori_loop(1, GROUP + 1, step, 0)
-        if head < 2:
-            totals_step(2 * HEADS + head)
-
-    for array in range(3):
-        drain(targets[array].at[:, pl.ds(0, BLOCK - STRIP), :], in_send.at[array])
-    for array in range(2):
-        drain_halo(array)
-    for number, slots, size in ((0, slots_a, GROUP), (1, slots_b, NY)):
-        drain(slots.at[pl.ds(0, size - 1)], stat_send.at[number])
-    for number in range(NZ - 1):
-        relay_drain(number)
+
+        @pl.when(head == 0)
+        def _():
+            relay_wait(NZ - 3)
+            relay_start(NZ - 2)
+
+        @pl.when(head == 1)
+        def _():
+            relay_wait(NZ - 2)
+            totals_end()
+
+        @pl.when(head == 2)
+        def _():
+            for array in range(2):
+                drain(targets[array].at[:, pl.ds(0, BLOCK - STRIP), :], in_send.at[array])
+                drain_halo(array)
+            for number, slots, size in ((0, slots_a, GROUP), (1, slots_b, NY)):
+                drain(slots.at[pl.ds(0, size - 1)], stat_send.at[number])
+
+            def relays_out(number, carry):
+                relay_drain(number)
+                return carry
+
+            lax.fori_loop(0, NZ - 1, relays_out, 0)
+
+        return carry
+
+    lax.fori_loop(0, HEADS, one_head, 0)
+    drain(q_buf.at[:, pl.ds(0, BLOCK - STRIP), :], in_send.at[2])
     drain(o_buf.at[:, pl.ds(0, BLOCK - STRIP), :], out_send)
     drain(out_ref, out_recv)
 
@@ -493,6 +565,8 @@
             pltpu.VMEM((NZ, 8, LANES), jnp.float32),
             pltpu.VMEM((1, STRIP), jnp.int32),
             pltpu.VMEM((1, STRIP), jnp.float32),
+            pltpu.VMEM((3,) + queries.shape, jnp.bfloat16),
+            pltpu.SemaphoreType.DMA((3,)),
             pltpu.SemaphoreType.DMA((4,)),
             pltpu.SemaphoreType.DMA((3,)),
             pltpu.SemaphoreType.DMA((3, HEADS)),

time: 77.7 us -> 77.7 us (level); the launches traced: 76.4 us -> 77.4 us
  Pallas kernels: 75.8 us -> 76.8 us
    pallas_call x1, Pallas kernels: 74.6 us -> 75.6 us  [per_device(): pl.pallas_call(kernel, name='exchange_and_attend', out_shape=(pltpu.VMEM(...]
where the time goes in v5:
time: 77.7 us; the launch traced here: 77.4 us
  Pallas kernels  76.8 us (99%)
    pallas_call x1, Pallas kernels, per_device(): pl.pallas_call(kernel, name='exchange_and_attend', out_shape=(pltpu.VMEM(...  75.6 us

profile of v5, /device:TPU:1, one launch (start us, length us, event | category | flops | bytes accessed | tf_op | source)
XLA Modules:
  0.0 77.4 jit_solution(1521204191318517743)
XLA Ops:
  0.6 75.6 %exchange_and_attend.1 = (bf16[192,4096]{1,0:T(8,128)(2,1)S(1)}, f32[1,128]{1,0:T(1,128)S(1)}, f32[1,128]{1,0:T(1,128)S(1)}) custom-call(bf16[192,4096]{1,0:T(8,128)(2,1)} %q_hbm.1, bf16[192,4096]{1,0:T(8,128)(2,1)} %k_hbm.1, bf16[192,4096]{1,0:T(8,128)(2,1)} %v_hbm.1, s32[384,128]{1,0:T(8,128)} %bitcast.6, s32[384,128]{1,0:T(8,128)} %bitcast.7, ...), custom_call_target="tpu_custom_call" | custom-call | tf_op jit(solution)/shard_map/exchange_and_attend/pallas_call | solution.py:543
  76.2 1.2 %store_results.1 = (bf16[192,4096]{1,0:T(8,128)(2,1)}, f32[1,128]{1,0:T(1,128)}, f32[1,128]{1,0:T(1,128)}) custom-call(bf16[192,4096]{1,0:T(8,128)(2,1)S(1)} %get-tuple-element.9.attended, f32[1,128]{1,0:T(1,128)S(1)} %get-tuple-element.10.counts, f32[1,128]{1,0:T(1,128)S(1)} %get-tuple-element.11.losses), custom_call_target="tpu_custom_call" | custom-call | tf_op jit(solution)/shard_map/store_results/pallas_call | solution.py:526

commit v6 on v5

--- a/solution.py
+++ b/solution.py
@@ -165,7 +165,7 @@
             ).start()
 
         def near(o, carry):
-            send(toward(1 + (NX - 2) * lax.rem(o, 2), lax.div(o, 2)))
+            send(toward(1 + (NX - 2) * lax.rem(o + c, 2), lax.div(o, 2)))
             return carry
 
         def far(o, carry):
@@ -469,7 +469,7 @@
 
         def step(i, carry):
             j = i - 1
-            steps = jnp.where(j < 2, 2, jnp.where(j < 6, 1 + (NX - 2) * lax.rem(j, 2), 0))
+            steps = jnp.where(j < 2, 2, jnp.where(j < 6, 1 + (NX - 2) * lax.rem(j + c, 2), 0))
             other = jnp.where(j < 2, j, jnp.where(j < 6, lax.div(j - 2, 2), 1 - lax.rem(j, 2)))
             attend(head, toward(steps, other))
             return carry

time: 77.7 us -> 77.7 us (level)
  no operation moved by 1% of the time
where the time goes in v6:
time: 77.7 us; the launch traced here: 77.4 us
  Pallas kernels  76.8 us (99%)
    pallas_call x1, Pallas kernels, per_device(): pl.pallas_call(kernel, name='exchange_and_attend', out_shape=(pltpu.VMEM(...  75.6 us

profile of v6, /device:TPU:1, one launch (start us, length us, event | category | flops | bytes accessed | tf_op | source)
XLA Modules:
  0.0 77.4 jit_solution(9803692758121237366)
XLA Ops:
  0.6 75.6 %exchange_and_attend.1 = (bf16[192,4096]{1,0:T(8,128)(2,1)S(1)}, f32[1,128]{1,0:T(1,128)S(1)}, f32[1,128]{1,0:T(1,128)S(1)}) custom-call(bf16[192,4096]{1,0:T(8,128)(2,1)} %q_hbm.1, bf16[192,4096]{1,0:T(8,128)(2,1)} %k_hbm.1, bf16[192,4096]{1,0:T(8,128)(2,1)} %v_hbm.1, s32[384,128]{1,0:T(8,128)} %bitcast.6, s32[384,128]{1,0:T(8,128)} %bitcast.7, ...), custom_call_target="tpu_custom_call" | custom-call | tf_op jit(solution)/shard_map/exchange_and_attend/pallas_call | solution.py:543
  76.3 1.2 %store_results.1 = (bf16[192,4096]{1,0:T(8,128)(2,1)}, f32[1,128]{1,0:T(1,128)}, f32[1,128]{1,0:T(1,128)}) custom-call(bf16[192,4096]{1,0:T(8,128)(2,1)S(1)} %get-tuple-element.9.attended, f32[1,128]{1,0:T(1,128)S(1)} %get-tuple-element.10.counts, f32[1,128]{1,0:T(1,128)S(1)} %get-tuple-element.11.losses), custom_call_target="tpu_custom_call" | custom-call | tf_op jit(solution)/shard_map/store_results/pallas_call | solution.py:526

commit v7 on v5

--- a/solution.py
+++ b/solution.py
@@ -431,6 +431,15 @@
 
         def spread(head, carry, array=array):
             wait_group(array, head)
+            @pl.when(head == 0)
+            def _():
+                start_group(array, HEADS - 1)
+                stage_copies[array + 1].wait()
+
+            @pl.when(head > 0)
+            def _():
+                start_group(array + 1, head - 1)
+
             if array == 0:
 
                 @pl.when((head == 0) & (from_upper > 0))
@@ -438,15 +447,6 @@
                     pl.semaphore_wait(met_upper, from_upper)
 
             start_halo(array, head)
-
-            @pl.when(head == 0)
-            def _():
-                start_group(array, HEADS - 1)
-                stage_copies[array + 1].wait()
-
-            @pl.when(head > 0)
-            def _():
-                start_group(array + 1, head - 1)
 
             if array == 0:
                 totals_start(head)

time: 77.7 us -> 77.7 us (level)
  no operation moved by 1% of the time
where the time goes in v7:
time: 77.7 us; the launch traced here: 77.4 us
  Pallas kernels  76.8 us (99%)
    pallas_call x1, Pallas kernels, per_device(): pl.pallas_call(kernel, name='exchange_and_attend', out_shape=(pltpu.VMEM(...  75.6 us

profile of v7, /device:TPU:1, one launch (start us, length us, event | category | flops | bytes accessed | tf_op | source)
XLA Modules:
  0.0 77.4 jit_solution(6532653873001223852)
XLA Ops:
  0.6 75.6 %exchange_and_attend.1 = (bf16[192,4096]{1,0:T(8,128)(2,1)S(1)}, f32[1,128]{1,0:T(1,128)S(1)}, f32[1,128]{1,0:T(1,128)S(1)}) custom-call(bf16[192,4096]{1,0:T(8,128)(2,1)} %q_hbm.1, bf16[192,4096]{1,0:T(8,128)(2,1)} %k_hbm.1, bf16[192,4096]{1,0:T(8,128)(2,1)} %v_hbm.1, s32[384,128]{1,0:T(8,128)} %bitcast.6, s32[384,128]{1,0:T(8,128)} %bitcast.7, ...), custom_call_target="tpu_custom_call" | custom-call | tf_op jit(solution)/shard_map/exchange_and_attend/pallas_call | solution.py:543
  76.2 1.2 %store_results.1 = (bf16[192,4096]{1,0:T(8,128)(2,1)}, f32[1,128]{1,0:T(1,128)}, f32[1,128]{1,0:T(1,128)}) custom-call(bf16[192,4096]{1,0:T(8,128)(2,1)S(1)} %get-tuple-element.9.attended, f32[1,128]{1,0:T(1,128)S(1)} %get-tuple-element.10.counts, f32[1,128]{1,0:T(1,128)S(1)} %get-tuple-element.11.losses), custom_call_target="tpu_custom_call" | custom-call | tf_op jit(solution)/shard_map/store_results/pallas_call | solution.py:526
